TPU v7x, 32 devices: a whole 2x2x4 slice. The times are simulated.
32 devices in a mesh: ep: 8 (over z, x), tp: 4 (over y, core).
Axes of the slice: x: 2, y: 2, z: 4, core: 2. Of those that a mesh axis runs over, the one named last changes fastest.
Arguments:
- query_latent: bfloat16 [128, 64, 512], P('ep', 'tp'), may hold values from -50 to 50
- query_rope: bfloat16 [128, 64, 64], P('ep', 'tp'), may hold values from -5 to 5
- cache_latent: bfloat16 [128, 256, 512], P('ep'), may hold values from -6 to 6
- cache_rope: bfloat16 [128, 64, 256], P('ep'), may hold values from -5 to 5
- cache_lengths: int32 [128], P('ep'), may hold values from 2 to 256
- value_up: bfloat16 [64, 512, 128], P('tp'), may hold values from -0.25 to 0.25
- out_proj: bfloat16 [3584, 8192], P('ep', 'tp'), may hold values from -0.0625 to 0.0625
- residual: bfloat16 [128, 3584], P('ep'), may hold values from -6 to 6
- norm_gain: float32 [3584], replicated, may hold values from 0.1 to 1.9
- router: bfloat16 [3584, 8], replicated, may hold values from -0.09375 to 0.09375
- trainer_gate: bfloat16 [8, 3584, 1024], P('ep', None, 'tp'), may hold values from -0.09375 to 0.09375
- trainer_up: bfloat16 [8, 3584, 1024], P('ep', None, 'tp'), may hold values from -0.09375 to 0.09375
- trainer_down: bfloat16 [8, 1024, 3584], P('ep', 'tp'), may hold values from -0.1875 to 0.1875
- hot_experts: int32 [2], replicated, may hold values from 0 to 7, as said below
- replica_index: int32 [8], replicated, may hold values from 0 to 1, as said below
- token_experts: int32 [128, 8], P('ep'), may hold values from 0 to 7, as said below
- replica_pick: int32 [128, 8], P('ep'), may hold values from 0 to 1048575
Outputs:
- layer_out: bfloat16 [128, 3584], P('ep', 'tp')
Inputs may be any that keep to these rules, and one draw needn't show every extreme that they name: `hot_experts`: the 2 hot experts differ, and the largest of them is 7. `replica_index`: the group right after the trainer of each hot expert (next index of ep, wrapping) holds a replica of that expert. `token_experts`: the 8 experts of one row differ, and every row names all hot experts.
All inputs are finite; a program needn't handle non-finite values.
Results may differ from a plain program's by a relative error of at most 0.008.
Values may be sent and summed in bfloat16 or wider, within the bound.
No kernel may reach another device: no remote copies, remote signals or barrier semaphores. Data moves between devices by JAX's collectives and lax.ppermute only.
A program may use at most 128 MiB of HBM per device.

v0:
```python
import jax
import jax.numpy as jnp
from jax import lax
from jax.sharding import PartitionSpec as P

D = 3584
TOPK = 8
SLOT_DEV = 2
CAP = 2
HOT = 2


score_scale = 192.0 ** (-0.5)
route_scale = 2.5
norm_eps = 1e-06


def spread(block, axis, owner):
    block = jnp.where(lax.axis_index(axis) == owner, block, jnp.zeros_like(block))
    return lax.psum(block, axis)


def choose_slots(expert_flat, pick_flat, hot_experts, replica_index, groups):
    slot_count = groups * SLOT_DEV
    slot_ids = lax.iota(jnp.int32, slot_count)
    owner_group = slot_ids // SLOT_DEV
    column = slot_ids % SLOT_DEV
    group_ids = lax.iota(jnp.int32, groups)
    owner_pick = jnp.sum(
        jnp.where(owner_group[:, None] == group_ids[None, :], replica_index[None, :], 0), axis=1
    )
    hot_ids = lax.iota(jnp.int32, HOT)
    owner_hot = jnp.sum(
        jnp.where(owner_pick[:, None] == hot_ids[None, :], hot_experts[None, :], 0), axis=1
    )
    slot_expert = jnp.where(column == 0, owner_group, owner_hot)
    holding = (expert_flat[:, None] == slot_expert[None, :]).astype(jnp.int32)
    holders = jnp.sum(holding, axis=1)
    candidate_rank = jnp.cumsum(holding, axis=1) - 1
    target = pick_flat % holders
    chosen = holding * (candidate_rank == target[:, None]).astype(jnp.int32)
    return (chosen, slot_expert)


def attend(query_latent, query_rope, cache_latent, cache_rope, cache_lengths, value_up):
    latent_term = jnp.einsum(
        "bhl,bpl->bhp", query_latent, cache_latent, preferred_element_type=jnp.float32
    )
    rope_term = jnp.einsum(
        "bhr,brp->bhp", query_rope, cache_rope, preferred_element_type=jnp.float32
    )
    scores = (latent_term + rope_term) * score_scale
    places = lax.broadcasted_iota(jnp.int32, scores.shape, 2)
    in_range = places < cache_lengths[:, None, None]
    scores = jnp.where(in_range, scores, -1e30)
    row_max = jnp.max(scores, axis=2, keepdims=True)
    shifted = jnp.where(in_range, jnp.exp(scores - row_max), 0.0)
    probs_bf = (shifted / jnp.sum(shifted, axis=2, keepdims=True)).astype(jnp.bfloat16)
    latent_out = jnp.einsum(
        "bhp,bpl->bhl", probs_bf, cache_latent, preferred_element_type=jnp.float32
    ).astype(jnp.bfloat16)
    head_values = jnp.einsum(
        "bhl,hlv->bhv", latent_out, value_up, preferred_element_type=jnp.float32
    ).astype(jnp.bfloat16)
    return head_values.reshape(head_values.shape[0], -1)


def per_device(
    query_latent,
    query_rope,
    cache_latent,
    cache_rope,
    cache_lengths,
    value_up,
    out_proj,
    residual,
    norm_gain,
    router,
    trainer_gate,
    trainer_up,
    trainer_down,
    hot_experts,
    replica_index,
    token_experts,
    replica_pick,
):
    groups = lax.axis_size("ep")
    model_width = residual.shape[1]
    part_width = model_width // lax.axis_size("tp")
    col_start = lax.axis_index("tp") * part_width
    own_gate = trainer_gate[0]
    own_up = trainer_up[0]
    own_down = trainer_down[0]
    group_ids = lax.iota(jnp.int32, groups)
    my_replica = jnp.sum(jnp.where(group_ids == lax.axis_index("ep"), replica_index, 0))
    spare_gate = jnp.zeros_like(own_gate)
    spare_up = jnp.zeros_like(own_up)
    spare_down = jnp.zeros_like(own_down)
    for hot_rank in range(HOT):
        got_gate, got_up, got_down = (
            spread(own_gate, "ep", hot_experts[hot_rank]),
            spread(own_up, "ep", hot_experts[hot_rank]),
            spread(own_down, "ep", hot_experts[hot_rank]),
        )
        taking = my_replica == hot_rank
        spare_gate = jnp.where(taking, got_gate, spare_gate)
        spare_up = jnp.where(taking, got_up, spare_up)
        spare_down = jnp.where(taking, got_down, spare_down)
    gate_slots = jnp.stack([own_gate, spare_gate])
    up_slots = jnp.stack([own_up, spare_up])
    down_slots = jnp.stack([own_down, spare_down])
    values_flat = attend(
        query_latent, query_rope, cache_latent, cache_rope, cache_lengths, value_up
    )
    column_part = lax.dot_general(
        lax.all_gather(values_flat, "ep", axis=0, tiled=True),
        out_proj,
        (((1,), (1,)), ((), ())),
        preferred_element_type=jnp.float32,
    )
    attn_part = lax.all_to_all(column_part, "ep", split_axis=0, concat_axis=1, tiled=True)
    attention = lax.psum_scatter(attn_part, "tp", scatter_dimension=1, tiled=True)
    hidden_part = (
        lax.dynamic_slice_in_dim(residual, col_start, part_width, 1).astype(jnp.float32) + attention
    )
    squares = lax.psum(jnp.sum(hidden_part * hidden_part, axis=1), "tp")
    root_mean = jnp.sqrt(squares / D + norm_eps)
    gain_part = lax.dynamic_slice_in_dim(norm_gain, col_start, part_width, 0)
    features = (hidden_part * gain_part[None, :] / root_mean[:, None]).astype(jnp.bfloat16)
    router_part = lax.dynamic_slice_in_dim(router, col_start, part_width, 0)
    logits = lax.psum(jnp.dot(features, router_part, preferred_element_type=jnp.float32), "tp")
    expert_ids = lax.iota(jnp.int32, logits.shape[1])
    picked = jnp.sum(
        jnp.where(token_experts[:, :, None] == expert_ids[None, None, :], logits[:, None, :], 0.0),
        axis=2,
    )
    affinity = jax.nn.sigmoid(picked)
    gates = route_scale * affinity / jnp.sum(affinity, axis=1, keepdims=True)
    tokens_here = token_experts.shape[0]
    chosen = choose_slots(
        token_experts.reshape(-1), replica_pick.reshape(-1), hot_experts, replica_index, groups
    )[0]
    earlier = jnp.cumsum(chosen, axis=0) - chosen
    prior = jnp.sum(earlier * chosen, axis=1)
    kept = prior < CAP
    depth_ids = lax.iota(jnp.int32, CAP)
    placed = chosen[:, :, None] * (
        (prior[:, None, None] == depth_ids[None, None, :]) & kept[:, None, None]
    ).astype(jnp.int32)
    placed = placed.reshape(tokens_here, TOPK, -1).astype(jnp.float32)
    dispatch = jnp.sum(placed, axis=1).astype(jnp.bfloat16)
    combine = jnp.sum(placed * gates[:, :, None], axis=1)
    outgoing = lax.dot_general(
        dispatch, features, (((0,), (0,)), ((), ())), preferred_element_type=jnp.float32
    ).astype(jnp.bfloat16)
    outgoing = outgoing.reshape(groups, SLOT_DEV * CAP, -1)
    row_count = groups * CAP
    arrived = lax.all_to_all(outgoing, "ep", split_axis=0, concat_axis=0, tiled=True)
    slot_rows = (
        arrived.reshape(groups, SLOT_DEV, CAP, -1)
        .transpose(1, 0, 2, 3)
        .reshape(SLOT_DEV, row_count, -1)
    )
    project_slot_rows = lax.all_gather(slot_rows, "tp", axis=2, tiled=True)
    gate_add = jnp.einsum(
        "srd,sdf->srf", project_slot_rows, gate_slots, preferred_element_type=jnp.float32
    )
    up_add = jnp.einsum(
        "srd,sdf->srf", project_slot_rows, up_slots, preferred_element_type=jnp.float32
    )
    gate_add, up_add = (gate_add, up_add)
    activated = (jax.nn.silu(gate_add) * up_add).astype(jnp.bfloat16)
    partial_value = jnp.einsum(
        "srf,sfd->srd", activated, down_slots, preferred_element_type=jnp.float32
    )
    expert_out = lax.psum_scatter(
        partial_value.astype(jnp.bfloat16), "tp", scatter_dimension=2, tiled=True
    )
    outbound = (
        expert_out.reshape(SLOT_DEV, groups, CAP, part_width)
        .transpose(1, 0, 2, 3)
        .reshape(groups, SLOT_DEV * CAP, part_width)
    )
    returned = lax.all_to_all(outbound, "ep", split_axis=0, concat_axis=0, tiled=True).reshape(
        -1, part_width
    )
    moe_part = jnp.dot(combine, returned.astype(jnp.float32), precision=lax.Precision.HIGHEST)
    return (hidden_part + moe_part).astype(jnp.bfloat16)


def solution(mesh):
    placed = (
        P("ep", "tp", None),
        P("ep", "tp", None),
        P("ep", None, None),
        P("ep", None, None),
        P("ep"),
        P("tp", None, None),
        P("ep", "tp"),
        P("ep", None),
        P(),
        P(),
        P("ep", None, "tp"),
        P("ep", None, "tp"),
        P("ep", "tp", None),
        P(),
        P(),
        P("ep", None),
        P("ep", None),
    )
    return jax.shard_map(
        per_device, mesh=mesh, in_specs=placed, out_specs=P("ep", "tp"), check_vma=False
    )
```

profile of v0, /device:TPU:0, one launch (start us, length us, event | category | flops | bytes accessed | tf_op | source)
XLA Modules:
  0.0 477.3 jit_solution(8051335654989066472)
XLA Ops:
  7.4 3.6 fusion.54
  11.0 0.2 fusion.16
  11.2 0.4 fusion.53
  11.6 2.9 convolution_convert_fusion.1
  14.5 0.5 fusion.17
  15.0 33.2 %all_gather.6 = bf16[128,2048]{1,0:T(8,128)(2,1)S(1)} all-gather(bf16[16,2048]{1,0:T(8,128)(2,1)S(1)} %bitcast.59), channel_id=1, replica_groups=mesh['ep'=8,'tp'=4] {'ep'}, dimensions={0}, use_global_device_ids=true | all-gather | bytes 589824 | tf_op jit(solution)/shard_map/all_gather | solution.py:116
  48.2 1.4 fusion.55
  49.6 5.6 %all-to-all-start = ((f32[8,16,448]{2,1,0:T(8,128)}), f32[8,16,448]{2,1,0:T(8,128)S(1)}, u32[]{:S(2)}, u32[]{:S(2)}) async-start(f32[8,16,448]{2,1,0:T(8,128)} %bitcast.1), calls=%async_computation | async-start | bytes 524288 | tf_op jit(solution)/shard_map/all_to_all | solution.py:121
  55.2 0.7 fusion.52
  57.2 5.1 %select_bitcast_fusion.4 = (bf16[3584,256]{1,0:T(8,128)(2,1)}, bf16[3584,256]{1,0:T(8,128)(2,1)}, bf16[3584,256]{1,0:T(8,128)(2,1)}, bf16[3584,256]{1,0:T(8,128)(2,1)}) fusion(bf16[1,3584,256]{2,1,0:T(8,128)(2,1)} %param.28, pred[]{:T(512)S(6)} %eq.152, pred[]{:T(512)S(6)} %eq.150, bf16[1,3584,256]{2,1,0:T(8,128)(2,1)} %param.27), kind=kLoop, calls=%fused_computation.17 | loop fusion | flops 3670016 | bytes 11010050 | tf_op jit(solution)/shard_map/jit(_where)/select_n | solution.py:19
  62.4 1.0 all-to-all-done
  63.4 0.2 copy.80
  63.6 0.8 all_to_all.23
  64.4 0.0 all-reduce.3.cloned.1.call-start
  64.5 3.6 select_bitcast_fusion.1
  68.1 0.6 copy-done.11
  68.7 0.1 copy.81
  68.8 0.1 eq.127
  68.9 0.1 select_reduce_fusion.1
  69.0 0.1 fusion.41
  69.1 0.1 compare_convert_fusion
  69.2 0.1 copy.82
  69.3 0.1 reshape.230
  69.4 0.1 fusion.40
  69.5 0.1 and_select_fusion
  69.6 0.1 fusion.39
  69.7 0.1 copy.83
  69.8 0.2 reduce_window_sum.23
  70.0 0.1 copy.84
  70.0 0.1 fusion.37
  70.2 0.2 convert_element_type.64
  70.3 0.8 dynamic_slice.10
  71.1 13.8 %reduce-scatter.5.cloned.1.call-done = f32[16,896]{1,0:T(8,128)} async-done(((f32[16,3584]{1,0:T(8,128)}), f32[16,896]{1,0:T(8,128)}) %reduce-scatter.5.cloned.1.call-update) | async-done | bytes 57360 | tf_op jit(solution)/shard_map/reduce_scatter | solution.py:122
  84.9 0.9 multiply_reduce_fusion.1
  85.8 6.1 %psum.56 = f32[16]{0:T(128)S(1)} all-reduce(f32[16]{0:T(128)S(1)} %multiply_reduce_fusion.1), channel_id=1, replica_groups=mesh['ep'=8,'tp'=4] {'tp'}, use_global_device_ids=true, to_apply=%region_10.11 | all-reduce | flops 16 | bytes 128 | tf_op jit(solution)/shard_map/psum | solution.py:126
  91.9 0.9 divide_convert_fusion.2
  92.8 0.8 fusion.35
  93.6 6.0 %psum.57 = f32[16,8]{0,1:T(8,128)S(1)} all-reduce(f32[16,8]{0,1:T(8,128)S(1)} %fusion.35), channel_id=1, replica_groups=mesh['ep'=8,'tp'=4] {'tp'}, use_global_device_ids=true, to_apply=%region_11.12 | all-reduce | flops 128 | bytes 1024 | tf_op jit(solution)/shard_map/psum | solution.py:131
  99.7 0.1 copy.85
  99.8 0.2 fusion.51
  100.0 0.1 convolution_convert_fusion.3
  100.2 0.6 reshape.231
  100.8 5.5 %all-to-all-start.1 = ((bf16[8,4,896]{2,1,0:T(4,128)(2,1)}), bf16[8,4,896]{2,1,0:T(4,128)(2,1)S(1)}, u32[]{:S(2)}, u32[]{:S(2)}) async-start(bf16[8,4,896]{2,1,0:T(4,128)(2,1)} %reshape.231), calls=%async_computation.2 | async-start | bytes 114688 | tf_op jit(solution)/shard_map/all_to_all | solution.py:158
  106.4 0.6 fusion.43
  108.3 5.8 %all-to-all-done.1 = bf16[8,4,896]{2,1,0:T(4,128)(2,1)S(1)} async-done(((bf16[8,4,896]{2,1,0:T(4,128)(2,1)}), bf16[8,4,896]{2,1,0:T(4,128)(2,1)S(1)}, u32[]{:S(2)}, u32[]{:S(2)}) %all-to-all-start.1) | async-done | bytes 57376 | tf_op jit(solution)/shard_map/all_to_all | solution.py:158
  114.2 5.7 %all_gather.7 = bf16[2,16,3584]{2,1,0:T(8,128)(2,1)S(1)} all-gather(bf16[2,16,896]{2,1,0:T(8,128)(2,1)S(1)} %reshape.233), channel_id=1, replica_groups=mesh['ep'=8,'tp'=4] {'tp'}, dimensions={2}, use_global_device_ids=true | all-gather | bytes 286720 | tf_op jit(solution)/shard_map/all_gather | solution.py:164
  119.9 291.9 %all-reduce.3.cloned.1.call-done = (bf16[256,3584]{1,0:T(8,128)(2,1)}, bf16[256,3584]{1,0:T(8,128)(2,1)}, bf16[3584,256]{1,0:T(8,128)(2,1)}, bf16[3584,256]{1,0:...) async-done(((bf16[256,3584]{1,0:T(8,128)(2,1)}, bf16[256,3584]{1,0:T(8,128)(2,1)}, bf16[3584,256]{1,0:T(8,128)(2,1)}, bf16[3584,256]{1,0:T(8,128)(2,1)}, ...) | async-done | bytes 11010064 | tf_op jit(solution)/shard_map/psum | solution.py:20
  411.8 1.8 select_bitcast_fusion.6
  413.6 0.2 copy-done.6
  413.9 0.6 fusion.1
  414.5 0.9 copy-done.4
  415.4 0.6 copy-done.5
  415.9 1.4 select_bitcast_fusion.3
  417.4 0.7 copy-done.2
  418.1 0.6 copy-done.3
  418.6 1.4 select_bitcast_fusion
  420.0 4.3 convolution_convert_fusion
  424.4 3.1 copy.91
  427.5 4.3 reshape.237
  431.8 23.1 %reduce-scatter.7.cloned.1.call-done = bf16[896,32]{1,0:T(8,128)(2,1)} async-done(((bf16[3584,32]{1,0:T(8,128)(2,1)}), bf16[896,32]{1,0:T(8,128)(2,1)}) %reduce-scatter.7.cloned.1.call-update) | async-done | bytes 57360
  454.9 1.2 reshape.238
  456.1 0.7 copy.87
  456.8 12.1 %all_to_all.29 = bf16[8,4,896]{2,1,0:T(4,128)(2,1)S(1)} all-to-all(bf16[8,4,896]{2,1,0:T(4,128)(2,1)S(1)} %copy.89), channel_id=1, replica_groups=mesh['ep'=8,'tp'=4] {'ep'}, dimensions={0} | all-to-all | bytes 114688 | tf_op jit(solution)/shard_map/all_to_all | solution.py:184
  469.0 0.8 fusion.18
  (48 shorter events, 0.5 us)
Async XLA Ops:
  7.4 7.1 %copy-start = (bf16[16,512,128]{2,1,0:T(8,128)(2,1)S(1)}, bf16[16,512,128]{2,1,0:T(8,128)(2,1)}, u32[]{:S(2)}) copy-start(bf16[16,512,128]{2,1,0:T(8,128)(2,1)} %param.22) | copy-start | bytes 6291460
  7.4 3.6 copy-start.9
  7.4 3.6 copy-start.7
  7.4 3.6 copy-start.13
  14.5 33.7 %copy-start.1 = (bf16[448,2048]{1,0:T(8,128)(2,1)S(1)}, bf16[448,2048]{1,0:T(8,128)(2,1)}, u32[]{:S(2)}) copy-start(bf16[448,2048]{1,0:T(8,128)(2,1)} %param.23) | copy-start | bytes 5505028
  15.0 40.2 %copy-start.14 = (s32[2]{0:T(128)S(1)}, s32[2]{0:T(128)}, u32[]{:S(2)}) copy-start(s32[2]{0:T(128)} %param.30) | copy-start | bytes 28
  49.6 13.8 %all-to-all-start = ((f32[8,16,448]{2,1,0:T(8,128)}), f32[8,16,448]{2,1,0:T(8,128)S(1)}, u32[]{:S(2)}, u32[]{:S(2)}) async-start(f32[8,16,448]{2,1,0:T(8,128)} %bitcast.1), calls=%async_computation | async-start | bytes 524288 | tf_op jit(solution)/shard_map/all_to_all | solution.py:121
  55.2 29.7 %reduce-scatter.5.cloned.1.call-start = ((), (), s32[]{:S(2)}) async-start(), calls=%async_computation.5 | async-start | bytes 286720 | tf_op jit(solution)/shard_map/reduce_scatter | solution.py:122
  64.4 347.4 %all-reduce.3.cloned.1.call-start = ((), (), s32[]{:S(2)}) async-start(), calls=%async_computation.7 | async-start | bytes 22020096 | tf_op jit(solution)/shard_map/psum | solution.py:20
  68.1 0.7 copy-start.11
  68.1 0.9 copy-start.15
  68.1 1.2 copy-start.12
  68.1 16.8 %copy-start.10 = (bf16[16,3584]{1,0:T(8,128)(2,1)S(1)}, bf16[16,3584]{1,0:T(8,128)(2,1)}, u32[]{:S(2)}) copy-start(bf16[16,3584]{1,0:T(8,128)(2,1)} %param.24) | copy-start | bytes 344068
  100.8 13.3 %all-to-all-start.1 = ((bf16[8,4,896]{2,1,0:T(4,128)(2,1)}), bf16[8,4,896]{2,1,0:T(4,128)(2,1)S(1)}, u32[]{:S(2)}, u32[]{:S(2)}) async-start(bf16[8,4,896]{2,1,0:T(4,128)(2,1)} %reshape.231), calls=%async_computation.2 | async-start | bytes 114688 | tf_op jit(solution)/shard_map/all_to_all | solution.py:158
  106.3 348.6 %reduce-scatter.7.cloned.1.call-start = ((), (), s32[]{:S(2)}) async-start(), calls=%async_computation.6 | async-start | bytes 1146880
  411.8 2.1 copy-start.6
  413.9 1.5 copy-start.4
  413.9 2.0 copy-start.5
  415.9 2.2 copy-start.2
  415.9 2.7 copy-start.3
  431.8 37.2 %copy-start.8 = (f32[16,896]{1,0:T(8,128)S(1)}, f32[16,896]{1,0:T(8,128)}, u32[]{:S(2)}) copy-start(f32[16,896]{1,0:T(8,128)} %reduce-scatter.5.cloned.1.call-done) | copy-start | bytes 172036
Sparse Core Ops, SparseCore 0:
  64.5 20.2 reduce-scatter.4
  431.9 22.9 reduce-scatter.6
Sparse Core Ops, SparseCore 1:
  69.9 341.8 all-reduce.2
where the time goes:
time: 478 us; the launch traced here: 477 us
  waiting for transfers between devices  336 us (70%)
  blocking collectives  63.1 us (13%)
  between operations  17.8 us (4%)
  other arithmetic  17.4 us (4%)
  local copies, waits for them, and re-layouts  16.8 us (4%)
  matrix products  15.3 us (3%)
  starting transfers between devices  11.3 us (2%)
    psum x1, waiting for transfers between devices, spread(): return lax.psum(block, axis)  292 us
    all_gather x1, blocking collectives, per_device(): lax.all_gather(values_flat, 'ep', axis=0, tiled=True)  33.2 us
    unnamed x4, waiting for transfers between devices  23.1 us
    reduce_scatter x1, waiting for transfers between devices, per_device(): lax.psum_scatter(attn_part, 'tp', scatter_dimension=1, tiled=True)  13.8 us
    unnamed x37, local copies, waits for them, and re-layouts  12.4 us
    all_to_all x1, blocking collectives, per_device(): lax.all_to_all(outbound, 'ep', split_axis=0, concat_axis=0, tiled=True)  12.1 us
  transfers between devices with their start and end apart: 5, of which 5 were waited for; matrix products, arithmetic and copies ran while one was open for 3% of the time, Pallas kernels for 0%

commit v1 on v0

v1 whole, which is shorter than its diff:
```python
import jax
import jax.numpy as jnp
from jax import lax
from jax.sharding import Mesh, PartitionSpec as P

TOPK = 8
SLOT_DEV = 2
CAP = 2
HOT = 2
CORES = 2
LANES = 128

score_scale = 192.0 ** (-0.5)
route_scale = 2.5
norm_eps = 1e-06
bf16 = jnp.bfloat16
f32 = jnp.float32


def choose_slots(expert_flat, pick_flat, hot_experts, replica_index, groups):
    slot_count = groups * SLOT_DEV
    slot_ids = lax.iota(jnp.int32, slot_count)
    owner_group = slot_ids // SLOT_DEV
    column = slot_ids % SLOT_DEV
    group_ids = lax.iota(jnp.int32, groups)
    owner_pick = jnp.sum(
        jnp.where(owner_group[:, None] == group_ids[None, :], replica_index[None, :], 0), axis=1
    )
    hot_ids = lax.iota(jnp.int32, HOT)
    owner_hot = jnp.sum(
        jnp.where(owner_pick[:, None] == hot_ids[None, :], hot_experts[None, :], 0), axis=1
    )
    slot_expert = jnp.where(column == 0, owner_group, owner_hot)
    holding = (expert_flat[:, None] == slot_expert[None, :]).astype(jnp.int32)
    holders = jnp.sum(holding, axis=1)
    candidate_rank = jnp.cumsum(holding, axis=1) - 1
    target = pick_flat % holders
    return holding * (candidate_rank == target[:, None]).astype(jnp.int32)


def keep_codes(token_experts, replica_pick, hot_experts, replica_index, groups, experts):
    chosen = choose_slots(
        token_experts.reshape(-1), replica_pick.reshape(-1), hot_experts, replica_index, groups
    )
    earlier = jnp.cumsum(chosen, axis=0) - chosen
    prior = jnp.sum(earlier * chosen, axis=1)
    code = 1.0 + (prior < CAP).astype(f32)
    expert_ids = lax.iota(jnp.int32, experts)
    named = token_experts[:, :, None] == expert_ids[None, None, :]
    return jnp.sum(jnp.where(named, code.reshape(token_experts.shape)[:, :, None], 0.0), axis=1)


def attend(query_latent, query_rope, cache_latent, cache_rope, cache_lengths, value_up):
    latent_term = jnp.einsum(
        "bhl,bpl->bhp", query_latent, cache_latent, preferred_element_type=f32
    )
    rope_term = jnp.einsum("bhr,brp->bhp", query_rope, cache_rope, preferred_element_type=f32)
    scores = (latent_term + rope_term) * score_scale
    places = lax.broadcasted_iota(jnp.int32, scores.shape, 2)
    in_range = places < cache_lengths[:, None, None]
    scores = jnp.where(in_range, scores, -1e30)
    row_max = jnp.max(scores, axis=2, keepdims=True)
    shifted = jnp.where(in_range, jnp.exp(scores - row_max), 0.0)
    probs_bf = (shifted / jnp.sum(shifted, axis=2, keepdims=True)).astype(bf16)
    latent_out = jnp.einsum(
        "bhp,bpl->bhl", probs_bf, cache_latent, preferred_element_type=f32
    ).astype(bf16)
    head_values = jnp.einsum(
        "bhl,hlv->bhv", latent_out, value_up, preferred_element_type=f32
    ).astype(bf16)
    return head_values.reshape(head_values.shape[0], -1)


def exchange(block, axis, size, mine):
    pieces = []
    for k in range(1, size):
        sent = lax.dynamic_index_in_dim(block, mine ^ k, 0, keepdims=False)
        pieces.append(lax.ppermute(sent, axis, [(i, i ^ k) for i in range(size)]))
    return lax.dynamic_index_in_dim(block, mine, 0, keepdims=False), pieces


def to_all(block, axes, count):
    spread = jnp.broadcast_to(block[None], (count,) + block.shape)
    return lax.all_to_all(spread, axes, split_axis=0, concat_axis=0, tiled=True)


def per_device(
    query_latent,
    query_rope,
    cache_latent,
    cache_rope,
    cache_lengths,
    value_up,
    out_proj,
    residual,
    norm_gain,
    router,
    trainer_gate,
    trainer_up,
    trainer_down,
    hot_experts,
    replica_index,
    token_experts,
    replica_pick,
):
    n_ep, n_y, n_c = lax.axis_size("ep"), lax.axis_size("y"), lax.axis_size("c")
    n_tp = n_y * n_c
    ep, y, c = lax.axis_index("ep"), lax.axis_index("y"), lax.axis_index("c")
    tp = y * n_c + c
    here, width = residual.shape
    tokens = here * n_ep
    quarter = tokens // n_tp
    experts = router.shape[1]
    block = out_proj.shape[0]
    sub = block // n_tp
    part = width // n_tp

    codes = keep_codes(
        token_experts, replica_pick, hot_experts, replica_index, n_ep, experts
    ).astype(bf16)
    shares = residual.reshape(here, n_ep, n_tp, sub)
    shares = lax.dynamic_index_in_dim(shares, tp, 2, keepdims=False).transpose(1, 0, 2)
    values = attend(
        query_latent, query_rope, cache_latent, cache_rope, cache_lengths, value_up
    )
    inner = values.shape[1]
    code_wide = -(-experts // LANES) * LANES
    sub_wide = -(-sub // LANES) * LANES
    parcel = jnp.concatenate(
        [
            jnp.broadcast_to(values[None], (n_ep, here, inner)),
            jnp.broadcast_to(
                jnp.pad(codes, ((0, 0), (0, code_wide - experts)))[None], (n_ep, here, code_wide)
            ),
            jnp.pad(shares, ((0, 0), (0, 0), (0, sub_wide - sub))),
        ],
        axis=2,
    )
    landed = lax.all_to_all(parcel, "ep", split_axis=0, concat_axis=0, tiled=True)
    landed = landed.reshape(tokens, -1)
    all_codes = landed[:, inner : inner + experts].astype(f32)
    all_shares = landed[:, inner + code_wide :]
    place = (
        lax.broadcasted_iota(jnp.int32, (sub_wide, block), 0) + tp * sub
        == lax.broadcasted_iota(jnp.int32, (sub_wide, block), 1)
    ) & (lax.broadcasted_iota(jnp.int32, (sub_wide, block), 0) < sub)
    column_part = lax.dot_general(
        landed[:, :inner], out_proj, (((1,), (1,)), ((), ())), preferred_element_type=f32
    ) + jnp.dot(all_shares, place.astype(bf16), preferred_element_type=f32)

    halves = column_part.reshape(n_y, n_c, quarter, block).transpose(1, 0, 2, 3)
    own, others = exchange(halves, "c", n_c, c)
    half = own + sum(others)
    own, others = exchange(half, "y", n_y, y)
    hidden_part = (own + sum(others)).astype(bf16)

    mine = to_all(hidden_part, ("ep", "y"), n_ep * n_y).reshape(n_ep, n_y, quarter, block)
    cores = [mine] + [
        lax.ppermute(mine, "c", [(i, i ^ k) for i in range(n_c)]) for k in range(1, n_c)
    ]
    ordered = []
    for j in range(n_c):
        pick = cores[0]
        for k in range(1, n_c):
            pick = jnp.where((c ^ k) == j, cores[k], pick)
        ordered.append(pick)
    rows = jnp.stack(ordered, axis=2).reshape(n_ep, tokens, block).transpose(1, 0, 2)
    hidden = rows.reshape(tokens, width).astype(f32)
    root_mean = jnp.sqrt(jnp.mean(hidden * hidden, axis=1, keepdims=True) + norm_eps)
    normed = (hidden * norm_gain[None, :] / root_mean).astype(bf16)
    logits = jnp.dot(normed, router, preferred_element_type=f32)
    affinity = jnp.where(all_codes > 0.5, jax.nn.sigmoid(logits), 0.0)
    gates = route_scale * affinity / jnp.sum(affinity, axis=1, keepdims=True)
    mine_only = lax.iota(jnp.int32, experts)[None, :] == ep
    weight = jnp.sum(
        jnp.where(mine_only & (all_codes > 1.5), gates, 0.0), axis=1, keepdims=True
    )

    gate_val = jnp.dot(normed, trainer_gate[0], preferred_element_type=f32)
    up_val = jnp.dot(normed, trainer_up[0], preferred_element_type=f32)
    act = (jax.nn.silu(gate_val) * up_val * weight).astype(bf16)
    partial = jnp.dot(act, trainer_down[0], preferred_element_type=f32).astype(bf16)

    split = partial.reshape(tokens, n_y, n_c, part).transpose(2, 1, 0, 3)
    own, others = exchange(split, "c", n_c, c)
    summed = own.astype(f32) + sum(o.astype(f32) for o in others)
    outbound = (
        summed.astype(bf16)
        .reshape(n_y, n_ep, here, part)
        .transpose(1, 0, 2, 3)
        .reshape(n_ep * n_y, here, part)
    )
    returned = lax.all_to_all(outbound, ("ep", "y"), split_axis=0, concat_axis=0, tiled=True)
    moe = jnp.sum(returned.astype(f32), axis=0)
    hidden_own = lax.dynamic_slice(hidden, (ep * here, tp * part), (here, part))
    return (hidden_own + moe).astype(bf16)


def solution(mesh):
    n_ep, n_tp = mesh.shape["ep"], mesh.shape["tp"]
    fine = Mesh(mesh.devices.reshape(n_ep, n_tp // CORES, CORES), ("ep", "y", "c"))
    tp = ("y", "c")
    placed = (
        P("ep", tp, None),
        P("ep", tp, None),
        P("ep", None, None),
        P("ep", None, None),
        P("ep"),
        P(tp, None, None),
        P("ep", tp),
        P("ep", None),
        P(),
        P(),
        P("ep", None, tp),
        P("ep", None, tp),
        P("ep", tp, None),
        P(),
        P(),
        P("ep", None),
        P("ep", None),
    )
    return jax.shard_map(
        per_device, mesh=fine, in_specs=placed, out_specs=P("ep", tp), check_vma=False
    )
```

time: 478 us -> 109 us (0.23)
  waiting for transfers between devices: 336 us -> 36.3 us
  blocking collectives: 63.1 us -> 18.8 us
  between operations: 17.8 us -> 0.36 us
  other arithmetic: 17.4 us -> 8.09 us
    psum x1 -> x0, waiting for transfers between devices: 292 us -> none  [spread(): return lax.psum(block, axis)]
    all_gather x2 -> x0, blocking collectives: 38.9 us -> none  [the longest x1 33.2 us: per_device(): lax.all_gather(values_flat, 'ep', axis=0, tiled=True)]
    unnamed x4 -> x0, waiting for transfers between devices: 23.1 us -> none
    all_to_all x2, waiting for transfers between devices: 6.79 us -> 28.7 us  [the longest x1 15.9 us: per_device(): lax.all_to_all(parcel, 'ep', split_axis=0, concat_axis=0, tiled=True)]
    reduce_scatter x1 -> x0, waiting for transfers between devices: 13.8 us -> none  [per_device(): lax.psum_scatter(attn_part, 'tp', scatter_dimension=1, tiled=True)]
    psum x2 -> x0, blocking collectives: 12.1 us -> none  [the longest x1 6.06 us: per_device(): squares = lax.psum(jnp.sum(hidden_part * hidden_part, axis=1), 'tp')]
    unnamed x37 -> x23, local copies, waits for them, and re-layouts: 12.4 us -> 1.93 us
    select_n x2 -> x0, other arithmetic: 8.71 us -> none  [spread(): jnp.where(lax.axis_index(axis) == owner, block, jnp.zeros_like(block))]
  transfers between devices with their start and end apart: 5 -> 6, of which waited for: 5 -> 6; matrix products, arithmetic and copies ran while one was open for 3% -> 1% of each run, Pallas kernels for 0% -> 0%
where the time goes in v1:
time: 109 us; the launch traced here: 108 us
  waiting for transfers between devices  36.3 us (33%)
  blocking collectives  18.8 us (17%)
  matrix products  16.5 us (15%)
  local copies, waits for them, and re-layouts  15 us (14%)
  starting transfers between devices  13 us (12%)
  other arithmetic  8.09 us (7%)
    all_to_all x1, blocking collectives, to_all(): return lax.all_to_all(spread, axes, split_axis=0, concat_axis=0, tiled=True)  18.8 us
    all_to_all x1, waiting for transfers between devices, per_device(): lax.all_to_all(parcel, 'ep', split_axis=0, concat_axis=0, tiled=True)  15.9 us
    all_to_all x1, waiting for transfers between devices, per_device(): lax.all_to_all(outbound, ('ep', 'y'), split_axis=0, concat_axis=0, tiled=...  12.8 us
    all_to_all x1, starting transfers between devices, per_device(): lax.all_to_all(parcel, 'ep', split_axis=0, concat_axis=0, tiled=True)  7.28 us
    ppermute x3, waiting for transfers between devices, exchange(): pieces.append(lax.ppermute(sent, axis, [(i, i ^ k) for i in range(size)]))  5.75 us
    dot_general x1, matrix products, per_device(): jnp.dot(act, trainer_down[0], preferred_element_type=f32).astype(bf16)  4.2 us
    all_to_all x1, starting transfers between devices, per_device(): lax.all_to_all(outbound, ('ep', 'y'), split_axis=0, concat_axis=0, tiled=...  3.89 us
    dot_general x1, matrix products, attend(): jnp.einsum('bhl,bpl->bhp', query_latent, cache_latent, preferred_element_...  3.51 us
  transfers between devices with their start and end apart: 6, of which 6 were waited for; matrix products, arithmetic and copies ran while one was open for 1% of the time, Pallas kernels for 0%

profile of v1, /device:TPU:0, one launch (start us, length us, event | category | flops | bytes accessed | tf_op | source)
XLA Modules:
  0.0 108.1 jit_solution(8059555495817769183)
XLA Ops:
  0.0 0.9 select_reduce_fusion.2
  0.9 0.7 fusion.54
  1.6 0.8 copy.75
  2.4 0.1 eq.103
  2.5 0.1 fusion.52
  2.6 0.1 compare_convert_fusion
  2.6 0.8 copy.76
  3.4 0.1 reshape.151
  3.5 0.1 and_select_fusion
  3.7 0.1 fusion.51
  3.7 0.1 copy.77
  3.8 0.2 reduce_window_sum.23
  4.0 0.1 copy.78
  4.1 0.1 fusion.50
  4.2 0.1 add.123
  4.3 0.1 copy.79
  4.3 0.7 select_reduce_fusion
  5.1 0.1 copy.96
  5.1 1.1 %reshape.152 = bf16[16,8,4,112]{3,2,1,0:T(4,128)(2,1)S(1)} reshape(bf16[16,3584]{1,0:T(8,128)(2,1)} %param.24) | data formatting | bytes 229376 | tf_op jit(solution)/shard_map/reshape | solution.py:121
  6.2 0.1 constant_dynamic-slice_fusion.1
  6.4 0.0 copy-start.6
  6.4 3.5 %fusion.61 = f32[16,16,256]{2,1,0:T(8,128)S(1)} fusion(bf16[16,16,512]{2,1,0:T(8,128)(2,1)} %param.17, bf16[16,256,512]{2,1,0:T(8,128)(2,1)} %param.19), kind=kOutput, calls=%fused_computation.105 | convolution fusion | flops 67108864 | bytes 4718592 | tf_op jit(solution)/shard_map/bhl,bpl->bhp/dot_general | solution.py:54
  9.9 0.2 fusion.14
  10.1 0.4 fusion.59
  10.5 2.9 %convolution_convert_fusion.1 = bf16[16,16,512]{2,1,0:T(8,128)(2,1)S(1)} fusion(bf16[16,256,512]{2,1,0:T(8,128)(2,1)} %param.19, f32[16,16]{1,0:T(8,128)S(1)} %fusion.59, f32[16,16,256]{2,1,0:T(8,128)S(1)} %fusion.14, s32[16]{0:T(128)S(1)} %copy-done.6), kind=kOutput, calls=%fused_computation.14 | convolution fusion | flops 67568128 | bytes 4719680 | tf_op jit(solution)/shard_map/bhp,bpl->bhl/dot_general | solution.py:65
  13.4 0.5 fusion.26
  14.0 0.9 fusion.32
  14.8 7.3 %all-to-all-start = ((bf16[8,16,2304]{2,1,0:T(8,128)(2,1)}), bf16[8,16,2304]{2,1,0:T(8,128)(2,1)S(1)}, u32[]{:S(2)}, u32[]{:S(2)}) async-start(bf16[8,16,2304]{2,1,0:T(8,128)(2,1)} %fusion.32), calls=%async_computation | async-start | bytes 1179648 | tf_op jit(solution)/shard_map/all_to_all | solution.py:139
  22.1 15.9 %all-to-all-done = bf16[8,16,2304]{2,1,0:T(8,128)(2,1)S(1)} async-done(((bf16[8,16,2304]{2,1,0:T(8,128)(2,1)}), bf16[8,16,2304]{2,1,0:T(8,128)(2,1)S(1)}, u32[]{:S(2)}, u32[]{:S(2)}) %all-to-all-start) | async-done | bytes 589856 | tf_op jit(solution)/shard_map/all_to_all | solution.py:139
  38.0 0.3 fusion.36
  38.3 2.1 %convolution_add_fusion.1 = f32[128,448]{0,1:T(8,128)S(1)} fusion(f32[128,448]{0,1:T(8,128)S(1)} %fusion.36, bf16[448,2048]{1,0:T(8,128)(2,1)} %param.23, bf16[128,2304]{1,0:T(8,128)(2,1)S(1)} %bitcast.93), kind=kOutput, calls=%fused_computation.22 | convolution fusion | flops 234938368 | bytes 2818048 | tf_op jit(solution)/shard_map/dot_general | solution.py:147
  40.5 0.1 copy.82
  40.7 0.1 collective-permute-start
  40.7 1.3 %collective-permute-done = f32[2,32,448]{2,1,0:T(8,128)S(1)} collective-permute-done((f32[2,32,448]{2,1,0:T(8,128)S(1)}, f32[2,32,448]{2,1,0:T(8,128)S(1)}, u32[]{:S(2)}, u32[]{:S(2)}) %collective-permute-start) | collective-permute-done | bytes 114720 | tf_op jit(solution)/shard_map/ppermute | solution.py:78
  42.1 1.6 %collective-permute-start.1 = (f32[32,448]{1,0:T(8,128)S(1)}, f32[32,448]{1,0:T(8,128)S(1)}, u32[]{:S(2)}, u32[]{:S(2)}) collective-permute-start(f32[32,448]{1,0:T(8,128)S(1)} %dynamic-slice_bitcast_fusion.1), channel_id=1, source_target_pairs={{0,2},{2,0},{1,3},{3,1},{4,6},{6,4},{5,7},{7,5},{8,10},{10,8},{9,1... | collective-permute-start | bytes 172040 | tf_op jit(solution)/shard_map/ppermute | solution.py:78
  43.7 2.7 %collective-permute-done.1 = f32[32,448]{1,0:T(8,128)S(1)} collective-permute-done((f32[32,448]{1,0:T(8,128)S(1)}, f32[32,448]{1,0:T(8,128)S(1)}, u32[]{:S(2)}, u32[]{:S(2)}) %collective-permute-start.1) | collective-permute-done | bytes 57376 | tf_op jit(solution)/shard_map/ppermute | solution.py:78
  46.5 18.8 %all_to_all.15 = bf16[16,32,448]{2,1,0:T(8,128)(2,1)S(1)} all-to-all(bf16[16,32,448]{2,1,0:T(8,128)(2,1)S(1)} %broadcast_in_dim.101), channel_id=1, replica_groups=mesh['ep'=8,'y'=2,'c'=2] {'ep','y'}, dimensions={0} | all-to-all | bytes 917504 | tf_op jit(solution)/shard_map/all_to_all | solution.py:84
  65.4 0.1 mul.75
  65.5 0.1 copy.93
  65.5 1.9 %collective-permute-done.2 = bf16[8,2,32,448]{3,2,1,0:T(8,128)(2,1)} collective-permute-done((bf16[8,2,32,448]{3,2,1,0:T(8,128)(2,1)S(1)}, bf16[8,2,32,448]{3,2,1,0:T(8,128)(2,1)}, u32[]{:S(2)}, u32[]{:S(2)}) %collective-permute-start.2) | collective-permute-done | bytes 458784 | tf_op jit(solution)/shard_map/ppermute | solution.py:159
  67.4 1.1 %select_bitcast_fusion.1 = (bf16[8,2,1,32,448]{4,3,1,0,2:T(8,128)(2,1)S(1)}, bf16[8,2,1,32,448]{4,3,1,0,2:T(8,128)(2,1)S(1)}) fusion(bf16[8,2,32,448]{3,2,1,0:T(8,128)(2,1)} %collective-permute-done.2, bf16[8,2,32,448]{3,2,1,0:T(8,128)(2,1)S(1)} %bitcast.96, pred[]{:T(512)S(6)} %eq.99, pred[]{:T(512)S(6)} %eq.118), kind=kLoop, calls=%fused_computation.40 | loop fusion | flops 458752 | bytes 1835010 | tf_op jit(solution)/shard_map/stack | solution.py:167
  68.5 0.2 maximum_convert_fusion
  68.7 0.3 copy.83
  69.0 0.2 fusion.1
  69.3 1.4 %fusion.3 = bf16[8,128,448]{2,1,0:T(8,128)(2,1)} fusion(f32[8,2,2,32,448]{4,3,2,1,0:T(8,128)S(1)} %copy.83, f32[128]{0:T(128)S(1)} %add_sqrt_fusion, f32[8,448]{1,0:T(8,128)S(1)} %mul.75), kind=kLoop, calls=%fused_computation.6 | loop fusion | flops 1376256 | bytes 2767360 | tf_op jit(solution)/shard_map/convert.6
  70.7 1.6 %copy.86 = bf16[128,8,448]{0,2,1:T(8,128)(2,1)S(1)} copy(bf16[128,8,448]{2,0,1:T(8,128)(2,1)} %bitcast.89) | data formatting | bytes 1835008 | tf_op jit(solution)/shard_map/div | solution.py:170
  72.2 2.8 %copy.84 = f32[128,8,448]{0,2,1:T(8,128)} copy(f32[128,8,448]{2,0,1:T(8,128)} %bitcast.86) | data formatting | bytes 3670016 | tf_op jit(solution)/shard_map/convert_element_type | solution.py:168
  75.1 2.1 %fusion.7 = f32[128,256]{1,0:T(8,128)S(1)} fusion(bf16[128,3584]{0,1:T(8,128)(2,1)S(1)} %bitcast.87, bf16[1,3584,256]{2,1,0:T(8,128)(2,1)} %param.27), kind=kOutput, calls=%fused_computation.10 | convolution fusion | flops 234881024 | bytes 2883584 | tf_op jit(solution)/shard_map/dot_general | solution.py:179
  77.2 0.7 fusion.60
  77.9 0.1 select_reduce_fusion.1
  78.0 4.2 %convolution_convert_fusion = bf16[128,3584]{1,0:T(8,128)(2,1)} fusion(bf16[1,256,3584]{2,1,0:T(8,128)(2,1)} %param.29, bf16[128,3584]{0,1:T(8,128)(2,1)S(1)} %bitcast.88, bf16[1,3584,256]{2,1,0:T(8,128)(2,1)} %param.28, f32[128,256]{1,0:T(8,128)S(1)} %fusion.7, f32[128]{0:T(128)S(1)} %select_reduce_fusion.1), kind=kOutput, calls=%fused_computation.1 | convolution fusion | flops 470450176 | bytes 5636608 | tf_op jit(solution)/shard_map/dot_general | solution.py:182
  82.2 2.5 %reshape.156 = bf16[128,2,2,896]{3,2,1,0:T(2,128)(2,1)S(1)} reshape(bf16[128,3584]{1,0:T(8,128)(2,1)} %convolution_convert_fusion) | data formatting | bytes 1835008 | tf_op jit(solution)/shard_map/reshape | solution.py:184
  84.6 1.9 %constant_dynamic-slice_fusion = (bf16[128,2,1,896]{3,2,1,0:T(2,128)(2,1)S(1)}, bf16[128,2,1,896]{3,2,1,0:T(2,128)(2,1)S(1)}) fusion(bf16[128,2,2,896]{3,2,1,0:T(2,128)(2,1)S(1)} %reshape.156, s32[]{:T(128)S(6)} %select_n.129, s32[]{:T(128)S(6)} %select_n.130), kind=kLoop, calls=%fused_computation.88 | loop fusion | bytes 1835016 | tf_op jit(solution)/shard_map/jit(dynamic_index_in_dim)/dynamic_slice | solution.py:79
  86.5 0.1 copy.104
  86.6 0.2 collective-permute-start.3
  86.8 1.7 %collective-permute-done.3 = bf16[2,128,896]{2,1,0:T(8,128)(2,1)S(1)} collective-permute-done((bf16[2,128,896]{2,1,0:T(8,128)(2,1)S(1)}, bf16[2,128,896]{2,1,0:T(8,128)(2,1)S(1)}, u32[]{:S(2)}, u32[]{:S(2)}) %collective-permute-start.3) | collective-permute-done | bytes 458784 | tf_op jit(solution)/shard_map/ppermute | solution.py:78
  88.5 0.1 fusion.31
  88.6 0.8 copy.90
  89.4 3.9 %all-to-all-start.2 = ((bf16[16,16,896]{2,1,0:T(8,128)(2,1)}), bf16[16,16,896]{2,1,0:T(8,128)(2,1)S(1)}, u32[]{:S(2)}, u32[]{:S(2)}) async-start(bf16[16,16,896]{2,1,0:T(8,128)(2,1)} %bitcast.26), calls=%async_computation.2 | async-start | bytes 917504 | tf_op jit(solution)/shard_map/all_to_all | solution.py:193
  93.3 1.2 %dynamic_slice.27 = f32[16,896]{0,1:T(8,128)S(1)} dynamic-slice(f32[128,3584]{0,1:T(8,128)} %bitcast.90, s32[]{:T(128)S(6)} %select_n.136, s32[]{:T(128)S(6)} %select_n.137), dynamic_slice_sizes={16,896} | dynamic-slice | bytes 114692 | tf_op jit(solution)/shard_map/dynamic_slice | solution.py:195
  94.5 0.2 copy.92
  94.7 12.8 %all-to-all-done.2 = bf16[16,16,896]{2,1,0:T(8,128)(2,1)S(1)} async-done(((bf16[16,16,896]{2,1,0:T(8,128)(2,1)}), bf16[16,16,896]{2,1,0:T(8,128)(2,1)S(1)}, u32[]{:S(2)}, u32[]{:S(2)}) %all-to-all-start.2) | async-done | bytes 458784 | tf_op jit(solution)/shard_map/all_to_all | solution.py:193
  107.4 0.1 convert_reduce_fusion
  107.5 0.6 add_convert_fusion
  (35 shorter events, 0.3 us)
Async XLA Ops:
  0.0 13.4 %copy-start = (bf16[16,512,128]{2,1,0:T(8,128)(2,1)S(1)}, bf16[16,512,128]{2,1,0:T(8,128)(2,1)}, u32[]{:S(2)}) copy-start(bf16[16,512,128]{2,1,0:T(8,128)(2,1)} %param.22) | copy-start | bytes 6291460
  6.4 3.6 %copy-start.3 = (bf16[16,64,256]{2,1,0:T(8,128)(2,1)S(1)}, bf16[16,64,256]{2,1,0:T(8,128)(2,1)}, u32[]{:S(2)}) copy-start(bf16[16,64,256]{2,1,0:T(8,128)(2,1)} %param.20) | copy-start | bytes 1572868
  6.4 3.5 %copy-start.4 = (bf16[16,16,64]{2,1,0:T(8,128)(2,1)S(1)}, bf16[16,16,64]{2,1,0:T(8,128)(2,1)}, u32[]{:S(2)}) copy-start(bf16[16,16,64]{2,1,0:T(8,128)(2,1)} %param.18) | copy-start | bytes 98308
  6.4 3.5 %copy-start.6 = (s32[16]{0:T(128)S(1)}, s32[16]{0:T(128)}, u32[]{:S(2)}) copy-start(s32[16]{0:T(128)} %param.21) | copy-start | bytes 196
  14.8 23.2 %all-to-all-start = ((bf16[8,16,2304]{2,1,0:T(8,128)(2,1)}), bf16[8,16,2304]{2,1,0:T(8,128)(2,1)S(1)}, u32[]{:S(2)}, u32[]{:S(2)}) async-start(bf16[8,16,2304]{2,1,0:T(8,128)(2,1)} %fusion.32), calls=%async_computation | async-start | bytes 1179648 | tf_op jit(solution)/shard_map/all_to_all | solution.py:139
  40.5 24.9 %copy-start.5 = (f32[3584]{0:T(1024)S(1)}, f32[3584]{0:T(1024)}, u32[]{:S(2)}) copy-start(f32[3584]{0:T(1024)} %param.25) | copy-start | bytes 43012
  40.7 1.4 %collective-permute-start = (f32[2,32,448]{2,1,0:T(8,128)S(1)}, f32[2,32,448]{2,1,0:T(8,128)S(1)}, u32[]{:S(2)}, u32[]{:S(2)}) collective-permute-start(f32[2,32,448]{2,1,0:T(8,128)S(1)} %dynamic-slice_bitcast_fusion), channel_id=1, source_target_pairs={{0,1},{1,0},{2,3},{3,2},{4,5},{5,4},{6,7},{7,6},{8,9},{9,8},{10,11... | collective-permute-start | bytes 344072 | tf_op jit(solution)/shard_map/ppermute | solution.py:78
  42.1 4.3 %collective-permute-start.1 = (f32[32,448]{1,0:T(8,128)S(1)}, f32[32,448]{1,0:T(8,128)S(1)}, u32[]{:S(2)}, u32[]{:S(2)}) collective-permute-start(f32[32,448]{1,0:T(8,128)S(1)} %dynamic-slice_bitcast_fusion.1), channel_id=1, source_target_pairs={{0,2},{2,0},{1,3},{3,1},{4,6},{6,4},{5,7},{7,5},{8,10},{10,8},{9,1... | collective-permute-start | bytes 172040 | tf_op jit(solution)/shard_map/ppermute | solution.py:78
  65.4 2.0 %collective-permute-start.2 = (bf16[8,2,32,448]{3,2,1,0:T(8,128)(2,1)S(1)}, bf16[8,2,32,448]{3,2,1,0:T(8,128)(2,1)}, u32[]{:S(2)}, u32[]{:S(2)}) collective-permute-start(bf16[8,2,32,448]{3,2,1,0:T(8,128)(2,1)S(1)} %bitcast.95), channel_id=1, source_target_pairs={{0,1},{1,0},{2,3},{3,2},{4,5},{5,4},{6,7},{7,6},{8,9},{9,8},{10,11... | collective-permute-start | bytes 1376264 | tf_op jit(solution)/shard_map/ppermute | solution.py:159
  69.0 1.7 %copy-start.1 = (f32[8,2,2,32,448]{4,3,2,1,0:T(8,128)}, f32[8,2,2,32,448]{4,3,2,1,0:T(8,128)S(1)}, u32[]{:S(2)}) copy-start(f32[8,2,2,32,448]{4,3,2,1,0:T(8,128)S(1)} %copy.83) | copy-start | bytes 5505028
  75.1 2.1 %copy-start.2 = (f32[128,8,448]{0,2,1:T(8,128)S(1)}, f32[128,8,448]{0,2,1:T(8,128)}, u32[]{:S(2)}) copy-start(f32[128,8,448]{0,2,1:T(8,128)} %copy.84) | copy-start | bytes 5505028
  75.1 2.1 %copy-start.7 = (bf16[3584,8]{0,1:T(8,128)(2,1)S(1)}, bf16[3584,8]{0,1:T(8,128)(2,1)}, u32[]{:S(2)}) copy-start(bf16[3584,8]{0,1:T(8,128)(2,1)} %param.26) | copy-start | bytes 172036
  86.6 1.9 %collective-permute-start.3 = (bf16[2,128,896]{2,1,0:T(8,128)(2,1)S(1)}, bf16[2,128,896]{2,1,0:T(8,128)(2,1)S(1)}, u32[]{:S(2)}, u32[]{:S(2)}) collective-permute-start(bf16[2,128,896]{2,1,0:T(8,128)(2,1)S(1)} %bitcast.100), channel_id=1, source_target_pairs={{0,1},{1,0},{2,3},{3,2},{4,5},{5,4},{6,7},{7,6},{8,9},{9,8},{10,11... | collective-permute-start | bytes 1376264 | tf_op jit(solution)/shard_map/ppermute | solution.py:78
  89.4 18.1 %all-to-all-start.2 = ((bf16[16,16,896]{2,1,0:T(8,128)(2,1)}), bf16[16,16,896]{2,1,0:T(8,128)(2,1)S(1)}, u32[]{:S(2)}, u32[]{:S(2)}) async-start(bf16[16,16,896]{2,1,0:T(8,128)(2,1)} %bitcast.26), calls=%async_computation.2 | async-start | bytes 917504 | tf_op jit(solution)/shard_map/all_to_all | solution.py:193

commit v2 on v1

v2 whole, which is shorter than its diff:
```python
import functools

import jax
import jax.numpy as jnp
from jax import lax
from jax.experimental import pallas as pl
from jax.experimental.pallas import tpu as pltpu
from jax.sharding import Mesh, PartitionSpec as P

TOPK = 8
SLOT_DEV = 2
CAP = 2
HOT = 2
CORES = 2
LANES = 128

score_scale = 192.0 ** (-0.5)
route_scale = 2.5
norm_eps = 1e-06
bf16 = jnp.bfloat16
f32 = jnp.float32


def keep_codes(token_experts, replica_pick, hot_experts, replica_index, experts):
    ids = lax.iota(jnp.int32, experts)
    held = jnp.where(
        replica_index[:, None] == lax.iota(jnp.int32, HOT)[None, :], hot_experts[None, :], 0
    ).sum(axis=1)
    count = 1 + jnp.sum((held[:, None] == ids[None, :]).astype(jnp.int32), axis=0)
    match = token_experts[:, :, None] == ids[None, None, :]
    named = jnp.any(match, axis=1)
    place = jnp.sum(jnp.where(match, replica_pick[:, :, None], 0), axis=1) % count[None, :]
    place = jnp.where(named, place, -1)
    tokens = lax.iota(jnp.int32, place.shape[0])
    ahead = (tokens[None, :] < tokens[:, None])[:, :, None] & (
        place[None, :, :] == place[:, None, :]
    )
    prior = jnp.sum(ahead.astype(jnp.int32), axis=1)
    return jnp.where(named, jnp.where(prior < CAP, 2.0, 1.0), 0.0)


def attend_kernel(
    steps, lengths, ql, qr, cl, cr, shares, vu_hbm, out, lat, vu, sem
):
    step = pl.program_id(0)
    per = ql.shape[0]
    heads = ql.shape[1]
    here = per * steps
    copy = pltpu.make_async_copy(vu_hbm, vu, sem)

    @pl.when(step == 0)
    def _():
        copy.start()

    for i in range(per):
        cache = cl[i]
        scores = lax.dot_general(
            ql[i], cache, (((1,), (1,)), ((), ())), preferred_element_type=f32
        )
        scores += jnp.dot(qr[i], cr[i], preferred_element_type=f32)
        scores *= score_scale
        places = lax.broadcasted_iota(jnp.int32, scores.shape, 1)
        live = places < lengths[step * per + i]
        scores = jnp.where(live, scores, -1e30)
        peak = jnp.max(scores, axis=1, keepdims=True)
        shifted = jnp.where(live, jnp.exp(scores - peak), 0.0)
        probs = (shifted / jnp.sum(shifted, axis=1, keepdims=True)).astype(bf16)
        mixed = jnp.dot(probs, cache, preferred_element_type=f32)
        for j in range(lat.shape[0]):
            lat[j, pl.ds((step * per + i) * heads, heads), :] = mixed[
                :, j * LANES : (j + 1) * LANES
            ]

    @pl.when(step == steps - 1)
    def _():
        copy.wait()
        vdim = vu.shape[2]
        for h in range(heads):
            rows = jnp.concatenate(
                [lat[j, pl.ds(h, here, stride=heads), :] for j in range(lat.shape[0])], axis=1
            ).astype(bf16)
            got = jnp.dot(rows, vu[h], preferred_element_type=f32).astype(bf16)
            for j in range(out.shape[0]):
                out[j, :, h * vdim : (h + 1) * vdim] = got
        for j in range(out.shape[0]):
            out[j, :, heads * vdim :] = shares[j]


def attend(query_latent, query_rope, cache_latent, cache_rope, lengths, value_up, shares):
    here, heads, latent = query_latent.shape
    rope, places = cache_rope.shape[1:]
    vdim = value_up.shape[2]
    dests, _, extra = shares.shape
    steps = 4
    per = here // steps
    spec = lambda *dims: pl.BlockSpec((per,) + dims, lambda t: (t,) + (0,) * len(dims))
    whole = lambda shape: pl.BlockSpec(shape, lambda t: (0,) * len(shape))
    out_shape = (dests, here, heads * vdim + extra)
    return pl.pallas_call(
        functools.partial(attend_kernel, steps),
        grid=(steps,),
        out_shape=jax.ShapeDtypeStruct(out_shape, bf16),
        in_specs=[
            pl.BlockSpec(memory_space=pltpu.SMEM),
            spec(heads, latent),
            spec(heads, rope),
            spec(places, latent),
            spec(rope, places),
            whole(shares.shape),
            pl.BlockSpec(memory_space=pl.ANY),
        ],
        out_specs=whole(out_shape),
        scratch_shapes=[
            pltpu.VMEM((latent // LANES, here * heads, LANES), f32),
            pltpu.VMEM(value_up.shape, bf16),
            pltpu.SemaphoreType.DMA,
        ],
        compiler_params=pltpu.CompilerParams(dimension_semantics=("arbitrary",)),
        name="attend",
    )(lengths, query_latent, query_rope, cache_latent, cache_rope, shares, value_up)


def expert_kernel(
    dims, where_ref, mine, other, gain, router, gate_hbm, up_hbm, down_hbm,
    keep_out, send_out, gate, up, down, x, codes, sems
):
    n_ep, n_y, quarter, block, experts, part = dims
    core, ep = where_ref[0], where_ref[1]
    half = n_y * quarter
    here = 2 * half // n_ep
    per_quarter = quarter // here
    copies = []
    for j in range(n_ep):
        rows = pl.ds(j * block, block)
        copies.append(
            (
                pltpu.make_async_copy(gate_hbm.at[rows], gate.at[rows], sems.at[0, j]),
                pltpu.make_async_copy(up_hbm.at[rows], up.at[rows], sems.at[1, j]),
            )
        )
    down_copy = pltpu.make_async_copy(down_hbm, down, sems.at[2, 0])
    for a, b in copies:
        a.start()
        b.start()
    down_copy.start()

    squares = jnp.zeros((2 * half, 1), f32)
    logits = jnp.zeros((2 * half, experts), f32)
    gate_val = jnp.zeros((2 * half, gate.shape[1]), f32)
    up_val = jnp.zeros((2 * half, up.shape[1]), f32)
    for j in range(n_ep):
        for i, src in enumerate((mine, other)):
            rows = src[:, j, :, :block].reshape(half, block).astype(f32)
            x[j, i * half : (i + 1) * half, :] = (rows * gain[:, j * block : (j + 1) * block]).astype(bf16)
        own = mine[:, j, :, :block].reshape(half, block).astype(f32)
        oth = other[:, j, :, :block].reshape(half, block).astype(f32)
        squares += jnp.concatenate(
            [jnp.sum(own * own, axis=1, keepdims=True), jnp.sum(oth * oth, axis=1, keepdims=True)], axis=0
        )
        y_of, rest = j // (per_quarter * 2), j % (per_quarter * 2)
        core_of, slot = rest // per_quarter, rest % per_quarter
        at = jnp.where(core == core_of, 0, half) + y_of * quarter + slot * here
        codes[pl.ds(pl.multiple_of(at, here), here), :] = mine[0, j, :here, block : block + experts].astype(f32)
        xj = x[j]
        a, b = copies[j]
        a.wait()
        b.wait()
        rows = slice(j * block, (j + 1) * block)
        gate_val += jnp.dot(xj, gate[rows, :], preferred_element_type=f32)
        up_val += jnp.dot(xj, up[rows, :], preferred_element_type=f32)
        logits += jnp.dot(xj, router[rows, :], preferred_element_type=f32)

    width = n_ep * block
    scale = 1.0 / jnp.sqrt(squares / width + norm_eps)
    code = codes[...]
    affinity = jnp.where(code > 0.5, jax.nn.sigmoid(logits * scale), 0.0)
    gates = route_scale * affinity / jnp.sum(affinity, axis=1, keepdims=True)
    mine_only = lax.broadcasted_iota(jnp.int32, gates.shape, 1) == ep
    weight = jnp.sum(
        jnp.where(mine_only & (code > 1.5), gates, 0.0), axis=1, keepdims=True
    )
    act = (jax.nn.silu(gate_val * scale) * (up_val * scale) * weight).astype(bf16)
    down_copy.wait()
    for flip, out in ((1, send_out), (0, keep_out)):
        to_core = jnp.where(core == 0, flip, 1 - flip)
        for y in range(n_y):
            cols = pl.ds(pl.multiple_of((y * 2 + to_core) * part, LANES), part)
            got = jnp.dot(act, down[:, cols], preferred_element_type=f32).astype(bf16)
            for i in range(2):
                of_core = jnp.where(core == 0, i, 1 - i)
                for q in range(n_y):
                    at = pl.multiple_of((q * 2 + of_core) * quarter, quarter)
                    src = i * half + q * quarter
                    out[y, pl.ds(at, quarter), :] = got[src : src + quarter, :]


def expert_block(where_ids, mine, other, gain, router, gate, up, down, block):
    n_y, n_ep, quarter, _ = mine.shape
    tokens = 2 * n_y * quarter
    experts = router.shape[1]
    part = down.shape[1] // (2 * n_y)
    dims = (n_ep, n_y, quarter, block, experts, part)
    vmem = pl.BlockSpec(memory_space=pltpu.VMEM)
    any_ = pl.BlockSpec(memory_space=pl.ANY)
    shape = jax.ShapeDtypeStruct((n_y, tokens, part), bf16)
    return pl.pallas_call(
        functools.partial(expert_kernel, dims),
        out_shape=(shape, shape),
        in_specs=[pl.BlockSpec(memory_space=pltpu.SMEM), vmem, vmem, vmem, vmem, any_, any_, any_],
        out_specs=(vmem, vmem),
        scratch_shapes=[
            pltpu.VMEM(gate.shape, bf16),
            pltpu.VMEM(up.shape, bf16),
            pltpu.VMEM(down.shape, bf16),
            pltpu.VMEM((n_ep, tokens, block), bf16),
            pltpu.VMEM((tokens, experts), f32),
            pltpu.SemaphoreType.DMA((3, n_ep)),
        ],
        name="experts",
    )(where_ids, mine, other, gain, router, gate, up, down)


def expert_plain(ep, c, mine, other, gain, router, gate, up, down, block):
    n_y, n_ep, quarter, _ = mine.shape
    tokens = 2 * n_y * quarter
    here = tokens // n_ep
    experts = router.shape[1]
    part = down.shape[1] // (2 * n_y)
    both = jnp.stack([jnp.where(c == 0, mine, other), jnp.where(c == 0, other, mine)], axis=1)
    codes = both[0, 0, :, :here, block : block + experts].reshape(tokens, experts).astype(f32)
    hidden = both[..., :block].transpose(0, 1, 3, 2, 4).reshape(tokens, -1).astype(f32)
    root_mean = jnp.sqrt(jnp.mean(hidden * hidden, axis=1, keepdims=True) + norm_eps)
    normed = (hidden * gain / root_mean).astype(bf16)
    logits = jnp.dot(normed, router, preferred_element_type=f32)
    affinity = jnp.where(codes > 0.5, jax.nn.sigmoid(logits), 0.0)
    gates = route_scale * affinity / jnp.sum(affinity, axis=1, keepdims=True)
    mine_only = lax.iota(jnp.int32, experts)[None, :] == ep
    weight = jnp.sum(jnp.where(mine_only & (codes > 1.5), gates, 0.0), axis=1, keepdims=True)
    gate_val = jnp.dot(normed, gate, preferred_element_type=f32)
    up_val = jnp.dot(normed, up, preferred_element_type=f32)
    act = (jax.nn.silu(gate_val) * up_val * weight).astype(bf16)
    partial = jnp.dot(act, down, preferred_element_type=f32).astype(bf16)
    split = partial.reshape(tokens, n_y, 2, part).transpose(2, 1, 0, 3)
    return (
        lax.dynamic_index_in_dim(split, c, 0, keepdims=False),
        lax.dynamic_index_in_dim(split, 1 - c, 0, keepdims=False),
    )


def exchange(block, axis, size, mine):
    pieces = []
    for k in range(1, size):
        sent = lax.dynamic_index_in_dim(block, mine ^ k, 0, keepdims=False)
        pieces.append(lax.ppermute(sent, axis, [(i, i ^ k) for i in range(size)]))
    return lax.dynamic_index_in_dim(block, mine, 0, keepdims=False), pieces


def swap_cores(block):
    return lax.ppermute(block, "c", [(0, 1), (1, 0)])


def per_device(
    query_latent,
    query_rope,
    cache_latent,
    cache_rope,
    cache_lengths,
    value_up,
    out_proj,
    residual,
    norm_gain,
    router,
    trainer_gate,
    trainer_up,
    trainer_down,
    hot_experts,
    replica_index,
    token_experts,
    replica_pick,
):
    n_ep, n_y, n_c = lax.axis_size("ep"), lax.axis_size("y"), lax.axis_size("c")
    n_tp = n_y * n_c
    ep, y, c = lax.axis_index("ep"), lax.axis_index("y"), lax.axis_index("c")
    tp = y * n_c + c
    here, width = residual.shape
    tokens = here * n_ep
    quarter = tokens // n_tp
    experts = router.shape[1]
    block = out_proj.shape[0]
    sub = block // n_tp
    part = width // n_tp

    sub_wide = -(-sub // LANES) * LANES
    shares = residual.reshape(here, n_ep, n_tp, sub)
    shares = lax.dynamic_index_in_dim(shares, tp, 2, keepdims=False).transpose(1, 0, 2)
    shares = jnp.pad(shares, ((0, 0), (0, 0), (0, sub_wide - sub)))
    parcel = attend(
        query_latent, query_rope, cache_latent, cache_rope, cache_lengths, value_up, shares
    )
    inner = parcel.shape[2] - sub_wide
    landed = lax.all_to_all(parcel, "ep", split_axis=0, concat_axis=0, tiled=True)
    landed = landed.reshape(tokens, -1)
    at_row = lax.broadcasted_iota(jnp.int32, (sub_wide, block), 0)
    at_col = lax.broadcasted_iota(jnp.int32, (sub_wide, block), 1)
    spot = ((at_row + tp * sub == at_col) & (at_row < sub)).astype(bf16)
    column_part = lax.dot_general(
        landed[:, :inner], out_proj, (((1,), (1,)), ((), ())), preferred_element_type=f32
    ) + jnp.dot(landed[:, inner:], spot, preferred_element_type=f32)

    halves = column_part.reshape(n_y, n_c, quarter, block).transpose(1, 0, 2, 3)
    own, others = exchange(halves, "c", n_c, c)
    half = own + sum(others)
    own, others = exchange(half, "y", n_y, y)
    hidden_part = (own + sum(others)).astype(bf16)

    codes = keep_codes(token_experts, replica_pick, hot_experts, replica_index, experts)
    codes = jnp.pad(codes.astype(bf16), ((0, quarter - here), (0, 0)))
    wide = -(-(block + experts) // LANES) * LANES
    sent = jnp.concatenate(
        [hidden_part, codes, jnp.zeros((quarter, wide - block - experts), bf16)], axis=1
    )
    count = n_y * n_ep
    mine = lax.all_to_all(
        jnp.broadcast_to(sent[None], (count, quarter, wide)),
        ("y", "ep"),
        split_axis=0,
        concat_axis=0,
        tiled=True,
    ).reshape(n_y, n_ep, quarter, wide)
    other = swap_cores(mine)

    gain = norm_gain[None, :]
    weights = (trainer_gate[0], trainer_up[0], trainer_down[0])
    if block % 16 == 0 and tokens <= 256:
        keep, send = expert_block(
            jnp.stack([c, ep]), mine, other, gain, router, *weights, block
        )
    else:
        keep, send = expert_plain(ep, c, mine, other, gain, router, *weights, block)

    got = swap_cores(send)
    summed = (keep.astype(f32) + got.astype(f32)).astype(bf16)
    outbound = summed.reshape(count, here, part)
    returned = lax.all_to_all(outbound, ("y", "ep"), split_axis=0, concat_axis=0, tiled=True)
    moe = jnp.sum(returned.astype(f32), axis=0)

    per_part = n_ep // n_tp
    first = ep * here
    of_tp, row = first // quarter, first % quarter
    cut = lambda a: lax.dynamic_slice(
        a, (of_tp // n_c, tp * per_part, row, 0), (1, per_part, here, block)
    )[0]
    hidden_own = jnp.where(of_tp % n_c == c, cut(mine), cut(other))
    hidden_own = hidden_own.transpose(1, 0, 2).reshape(here, part).astype(f32)
    return (hidden_own + moe).astype(bf16)


def solution(mesh):
    n_ep, n_tp = mesh.shape["ep"], mesh.shape["tp"]
    fine = Mesh(mesh.devices.reshape(n_ep, n_tp // CORES, CORES), ("ep", "y", "c"))
    tp = ("y", "c")
    placed = (
        P("ep", tp, None),
        P("ep", tp, None),
        P("ep", None, None),
        P("ep", None, None),
        P("ep"),
        P(tp, None, None),
        P("ep", tp),
        P("ep", None),
        P(),
        P(),
        P("ep", None, tp),
        P("ep", None, tp),
        P("ep", tp, None),
        P(),
        P(),
        P("ep", None),
        P("ep", None),
    )
    return jax.shard_map(
        per_device, mesh=fine, in_specs=placed, out_specs=P("ep", tp), check_vma=False
    )
```

time: 109 us -> 94 us (0.86)
  Pallas kernels: 0 us -> 17.1 us
  matrix products: 16.5 us -> 0.97 us
  local copies, waits for them, and re-layouts: 15 us -> 5.32 us
  waiting for transfers between devices: 36.3 us -> 33 us
  other arithmetic: 8.09 us -> 4.93 us
    pallas_call x0 -> x2, Pallas kernels: none -> 17.1 us  [the longest x1 10.6 us: attend(): pl.pallas_call(functools.partial(attend_kernel, steps), grid=(steps,), ou...]
    dot_general x8 -> x1, matrix products: 14.4 us -> 0.32 us  [per_device(): jnp.dot(landed[:, inner:], spot, preferred_element_type=f32)]
    reshape x3 -> x0, local copies, waits for them, and re-layouts: 3.35 us -> none  [the longest x1 2.45 us: per_device(): split = partial.reshape(tokens, n_y, n_c, part).transpose(2, 1, 0, 3)]
    dynamic_slice x2 -> x0, local copies, waits for them, and re-layouts: 3.11 us -> none  [the longest x1 1.9 us: exchange(): return (lax.dynamic_index_in_dim(block, mine, 0, keepdims=False), pieces)]
    convert_element_type x2, local copies, waits for them, and re-layouts: 3.1 us -> 0.18 us  [per_device(): hidden_own = hidden_own.transpose(1, 0, 2).reshape(here, part).astype(f32)]
    convert_element_type x3, other arithmetic: 0.34 us -> 2.7 us  [the longest x1 1.89 us: per_device(): summed = (keep.astype(f32) + got.astype(f32)).astype(bf16)]
    ppermute x3 -> x2, waiting for transfers between devices: 5.75 us -> 3.42 us  [exchange(): pieces.append(lax.ppermute(sent, axis, [(i, i ^ k) for i in range(size)]))]
    reduce_sum x7 -> x4, other arithmetic: 2.87 us -> 0.6 us  [the longest x1 0.41 us: keep_codes(): prior = jnp.sum(ahead.astype(jnp.int32), axis=1)]
  transfers between devices with their start and end apart: 6 -> 6, of which waited for: 6 -> 5; matrix products, arithmetic and copies ran while one was open for 1% -> 5% of each run, Pallas kernels for 0% -> 0%
where the time goes in v2:
time: 94 us; the launch traced here: 93.5 us
  waiting for transfers between devices  33 us (35%)
  blocking collectives  18.8 us (20%)
  Pallas kernels  17.1 us (18%)
  starting transfers between devices  13.1 us (14%)
  local copies, waits for them, and re-layouts  5.32 us (6%)
  other arithmetic  4.93 us (5%)
  matrix products  0.97 us (1%)
    all_to_all x1, blocking collectives, per_device(): lax.all_to_all(jnp.broadcast_to(sent[None], (count, quarter, wide)), ('y'...  18.8 us
    all_to_all x1, waiting for transfers between devices, per_device(): lax.all_to_all(parcel, 'ep', split_axis=0, concat_axis=0, tiled=True)  14.6 us
    all_to_all x1, waiting for transfers between devices, per_device(): lax.all_to_all(outbound, ('y', 'ep'), split_axis=0, concat_axis=0, tiled=...  13.3 us
    pallas_call x1, Pallas kernels, attend(): pl.pallas_call(functools.partial(attend_kernel, steps), grid=(steps,), ou...  10.6 us
    all_to_all x1, starting transfers between devices, per_device(): lax.all_to_all(parcel, 'ep', split_axis=0, concat_axis=0, tiled=True)  7.29 us
    pallas_call x1, Pallas kernels, expert_block(): pl.pallas_call(functools.partial(expert_kernel, dims), out_shape=(shape,...  6.44 us
    all_to_all x1, starting transfers between devices, per_device(): lax.all_to_all(outbound, ('y', 'ep'), split_axis=0, concat_axis=0, tiled=...  3.59 us
    ppermute x2, waiting for transfers between devices, exchange(): pieces.append(lax.ppermute(sent, axis, [(i, i ^ k) for i in range(size)]))  3.42 us
  transfers between devices with their start and end apart: 6, of which 5 were waited for; matrix products, arithmetic and copies ran while one was open for 5% of the time, Pallas kernels for 0%

profile of v2, /device:TPU:0, one launch (start us, length us, event | category | flops | bytes accessed | tf_op | source)
XLA Modules:
  0.0 93.5 jit_solution(10284919839343624239)
XLA Ops:
  0.0 0.0 copy-start
  0.0 1.2 %reshape.154 = bf16[16,8,4,112]{3,2,1,0:T(4,128)(2,1)S(1)} reshape(bf16[16,3584]{1,0:T(8,128)(2,1)} %param.24) | data formatting | bytes 229376 | tf_op jit(solution)/shard_map/reshape | solution.py:294
  1.2 0.1 constant_dynamic-slice_fusion
  1.3 0.6 pad.8.shares
  2.0 0.0 copy-start.7
  2.0 0.0 copy-start.8
  2.0 0.0 copy-start.4
  2.0 0.0 copy-start.6
  2.0 10.6 %attend.1 = bf16[8,16,2176]{2,1,0:T(8,128)(2,1)} custom-call(s32[16]{0:T(128)} %lengths.1, bf16[16,16,512]{2,1,0:T(8,128)(2,1)} %ql.1, bf16[16,16,64]{2,1,0:T(8,128)(2,1)} %qr.1, bf16[16,256,512]{2,1,0:T(8,128)(2,1)} %cl.1, bf16[16,64,256]{2,1,0:T(8,128)(2,1)} %cr.1, bf16[8,16,128]{2,1,0:T(8,128)(2,1)} %pad.8.shares, bf16[16,512,128]{2,1,0:T(8,128)(2,1)} %vu_hbm.1), custom_call_target="tpu_custom_call" | custom-call | tf_op jit(solution)/shard_map/attend/pallas_call | solution.py:99
  12.6 7.3 %all-to-all-start = ((bf16[8,16,2176]{2,1,0:T(8,128)(2,1)}), bf16[8,16,2176]{2,1,0:T(8,128)(2,1)S(1)}, u32[]{:S(2)}, u32[]{:S(2)}) async-start(bf16[8,16,2176]{2,1,0:T(8,128)(2,1)} %attend.1), calls=%async_computation | async-start | bytes 1114112 | tf_op jit(solution)/shard_map/all_to_all | solution.py:301
  19.9 0.0 copy-done.7
  19.9 0.0 copy-done.8
  19.9 0.1 fusion.14
  20.0 0.1 convert_reduce_fusion.2
  20.1 0.0 copy-done.4
  20.1 0.0 copy-done.6
  20.2 0.2 fusion.13
  20.4 0.1 copy.32
  20.5 14.6 %all-to-all-done = bf16[8,16,2176]{2,1,0:T(8,128)(2,1)S(1)} async-done(((bf16[8,16,2176]{2,1,0:T(8,128)(2,1)}), bf16[8,16,2176]{2,1,0:T(8,128)(2,1)S(1)}, u32[]{:S(2)}, u32[]{:S(2)}) %all-to-all-start) | async-done | bytes 557088 | tf_op jit(solution)/shard_map/all_to_all | solution.py:301
  35.1 0.3 fusion.2
  35.4 0.0 copy-done
  35.4 0.6 convolution_add_fusion
  36.1 0.0 copy-start.3
  36.1 0.1 copy.31
  36.2 0.0 copy-start.5
  36.3 0.1 collective-permute-start
  36.4 0.4 convert_reduce_fusion.1
  36.8 0.1 copy.33
  36.8 0.8 collective-permute-done
  37.7 1.6 %collective-permute-start.1 = (f32[32,448]{1,0:T(8,128)S(1)}, f32[32,448]{1,0:T(8,128)S(1)}, u32[]{:S(2)}, u32[]{:S(2)}) collective-permute-start(f32[32,448]{1,0:T(8,128)S(1)} %dynamic-slice_bitcast_fusion.1), channel_id=1, source_target_pairs={{0,2},{2,0},{1,3},{3,1},{4,6},{6,4},{5,7},{7,5},{8,10},{10,8},{9,1... | collective-permute-start | bytes 172040 | tf_op jit(solution)/shard_map/ppermute | solution.py:254
  39.3 0.1 copy.38
  39.4 0.1 pad.14.clone
  39.5 2.6 %collective-permute-done.1 = f32[32,448]{1,0:T(8,128)S(1)} collective-permute-done((f32[32,448]{1,0:T(8,128)S(1)}, f32[32,448]{1,0:T(8,128)S(1)}, u32[]{:S(2)}, u32[]{:S(2)}) %collective-permute-start.1) | collective-permute-done | bytes 57376 | tf_op jit(solution)/shard_map/ppermute | solution.py:254
  42.1 0.1 fusion.10
  42.2 18.8 %all_to_all.15 = bf16[16,32,512]{2,1,0:T(8,128)(2,1)S(1)} all-to-all(bf16[16,32,512]{2,1,0:T(8,128)(2,1)S(1)} %broadcast_in_dim.75), channel_id=1, replica_groups=mesh['ep'=8,'y'=2,'c'=2] {'y','ep'}, dimensions={0} | all-to-all | bytes 1048576 | tf_op jit(solution)/shard_map/all_to_all | solution.py:323
  61.0 0.0 copy-start.1
  61.0 0.0 collective-permute-start.2
  61.0 0.0 copy-done.3
  61.0 1.2 %copy.36.router = bf16[3584,8]{1,0:T(8,128)(2,1)} copy(bf16[3584,8]{0,1:T(8,128)(2,1)S(1)} %copy-done.3) | data formatting | bytes 114688 | tf_op args[9]
  62.3 0.0 copy-done.5
  62.3 0.6 broadcast_in_dim.76.gain
  62.9 0.6 pad_add_fusion.where_ref
  63.5 0.0 collective-permute-done.2.other
  63.5 0.0 copy-start.2
  63.5 0.0 copy-done.1
  63.5 0.8 copy-done.2
  64.3 6.4 %experts.1 = (bf16[2,128,896]{2,1,0:T(8,128)(2,1)}, bf16[2,128,896]{2,1,0:T(8,128)(2,1)}) custom-call(s32[2]{0:T(128)} %pad_add_fusion.where_ref, bf16[2,8,32,512]{3,2,1,0:T(8,128)(2,1)} %bitcast.31, bf16[2,8,32,512]{3,2,1,0:T(8,128)(2,1)} %copy-done.2, f32[1,3584]{1,0:T(1,128)} %broadcast_in_dim.76.gain, bf16[3584,8]{1,0:T(8,128)(2,1)} %copy.36.router, ...), custom_call_target="tpu_custom_call" | custom-call | tf_op jit(solution)/shard_map/experts/pallas_call | solution.py:206
  70.7 0.6 collective-permute-start.3
  71.3 1.7 %collective-permute-done.3 = bf16[2,128,896]{2,1,0:T(8,128)(2,1)S(1)} collective-permute-done((bf16[2,128,896]{2,1,0:T(8,128)(2,1)}, bf16[2,128,896]{2,1,0:T(8,128)(2,1)S(1)}, u32[]{:S(2)}, u32[]{:S(2)}) %collective-permute-start.3) | collective-permute-done | bytes 458784 | tf_op jit(solution)/shard_map/ppermute | solution.py:259
  72.9 1.9 %add_convert_fusion = bf16[2,128,896]{2,1,0:T(8,128)(2,1)} fusion(bf16[2,128,896]{2,1,0:T(8,128)(2,1)S(1)} %collective-permute-done.3, bf16[2,128,896]{2,1,0:T(8,128)(2,1)} %get-tuple-element.7), kind=kLoop, calls=%fused_computation.2 | loop fusion | flops 917504 | bytes 1376256 | tf_op jit(solution)/shard_map/convert_element_type | solution.py:342
  74.8 3.6 %all-to-all-start.2 = ((bf16[16,16,896]{2,1,0:T(8,128)(2,1)}), bf16[16,16,896]{2,1,0:T(8,128)(2,1)S(1)}, u32[]{:S(2)}, u32[]{:S(2)}) async-start(bf16[16,16,896]{2,1,0:T(8,128)(2,1)} %bitcast.16), calls=%async_computation.2 | async-start | bytes 917504 | tf_op jit(solution)/shard_map/all_to_all | solution.py:344
  78.5 0.8 convert_bitcast_fusion
  79.3 0.1 copy.35
  79.4 0.1 reshape.159
  79.5 13.3 %all-to-all-done.2 = bf16[16,16,896]{2,1,0:T(8,128)(2,1)S(1)} async-done(((bf16[16,16,896]{2,1,0:T(8,128)(2,1)}), bf16[16,16,896]{2,1,0:T(8,128)(2,1)S(1)}, u32[]{:S(2)}, u32[]{:S(2)}) %all-to-all-start.2) | async-done | bytes 458784 | tf_op jit(solution)/shard_map/all_to_all | solution.py:344
  92.8 0.1 convert_reduce_fusion
  92.9 0.6 add_convert_fusion.1
  (15 shorter events, 0.2 us)
Async XLA Ops:
  0.0 35.4 %copy-start = (bf16[448,2048]{1,0:T(8,128)(2,1)S(1)}, bf16[448,2048]{1,0:T(8,128)(2,1)}, u32[]{:S(2)}) copy-start(bf16[448,2048]{1,0:T(8,128)(2,1)} %param.23) | copy-start | bytes 5505028
  2.0 17.9 %copy-start.7 = (s32[2]{0:T(128)S(1)}, s32[2]{0:T(128)}, u32[]{:S(2)}) copy-start(s32[2]{0:T(128)} %param.30) | copy-start | bytes 28
  2.0 17.9 %copy-start.8 = (s32[8]{0:T(128)S(1)}, s32[8]{0:T(128)}, u32[]{:S(2)}) copy-start(s32[8]{0:T(128)} %param.31) | copy-start | bytes 100
  2.0 18.1 %copy-start.4 = (s32[16,8]{0,1:T(8,128)S(1)}, s32[16,8]{0,1:T(8,128)}, u32[]{:S(2)}) copy-start(s32[16,8]{0,1:T(8,128)} %param.32) | copy-start | bytes 1540
  2.0 18.1 %copy-start.6 = (s32[16,8]{0,1:T(8,128)S(1)}, s32[16,8]{0,1:T(8,128)}, u32[]{:S(2)}) copy-start(s32[16,8]{0,1:T(8,128)} %param.33) | copy-start | bytes 1540
  12.6 22.5 %all-to-all-start = ((bf16[8,16,2176]{2,1,0:T(8,128)(2,1)}), bf16[8,16,2176]{2,1,0:T(8,128)(2,1)S(1)}, u32[]{:S(2)}, u32[]{:S(2)}) async-start(bf16[8,16,2176]{2,1,0:T(8,128)(2,1)} %attend.1), calls=%async_computation | async-start | bytes 1114112 | tf_op jit(solution)/shard_map/all_to_all | solution.py:301
  36.1 24.9 %copy-start.3 = (bf16[3584,8]{0,1:T(8,128)(2,1)S(1)}, bf16[3584,8]{0,1:T(8,128)(2,1)}, u32[]{:S(2)}) copy-start(bf16[3584,8]{0,1:T(8,128)(2,1)} %param.26) | copy-start | bytes 172036
  36.2 26.0 %copy-start.5 = (f32[3584]{0:T(1024)S(1)}, f32[3584]{0:T(1024)}, u32[]{:S(2)}) copy-start(f32[3584]{0:T(1024)} %param.25) | copy-start | bytes 43012
  36.3 1.4 %collective-permute-start = (f32[2,32,448]{2,1,0:T(8,128)S(1)}, f32[2,32,448]{2,1,0:T(8,128)S(1)}, u32[]{:S(2)}, u32[]{:S(2)}) collective-permute-start(f32[2,32,448]{2,1,0:T(8,128)S(1)} %dynamic-slice_bitcast_fusion), channel_id=1, source_target_pairs={{0,1},{1,0},{2,3},{3,2},{4,5},{5,4},{6,7},{7,6},{8,9},{9,8},{10,11... | collective-permute-start | bytes 344072 | tf_op jit(solution)/shard_map/ppermute | solution.py:254
  37.7 4.3 %collective-permute-start.1 = (f32[32,448]{1,0:T(8,128)S(1)}, f32[32,448]{1,0:T(8,128)S(1)}, u32[]{:S(2)}, u32[]{:S(2)}) collective-permute-start(f32[32,448]{1,0:T(8,128)S(1)} %dynamic-slice_bitcast_fusion.1), channel_id=1, source_target_pairs={{0,2},{2,0},{1,3},{3,1},{4,6},{6,4},{5,7},{7,5},{8,10},{10,8},{9,1... | collective-permute-start | bytes 172040 | tf_op jit(solution)/shard_map/ppermute | solution.py:254
  61.0 2.5 %copy-start.1 = (bf16[16,32,512]{2,1,0:T(8,128)(2,1)}, bf16[16,32,512]{2,1,0:T(8,128)(2,1)S(1)}, u32[]{:S(2)}) copy-start(bf16[16,32,512]{2,1,0:T(8,128)(2,1)S(1)} %all_to_all.15) | copy-start | bytes 1572868
  61.0 2.5 %collective-permute-start.2 = (bf16[2,8,32,512]{3,2,1,0:T(8,128)(2,1)S(1)}, bf16[2,8,32,512]{3,2,1,0:T(8,128)(2,1)S(1)}, u32[]{:S(2)}, u32[]{:S(2)}) collective-permute-start(bf16[2,8,32,512]{3,2,1,0:T(8,128)(2,1)S(1)} %bitcast.30), channel_id=1, source_target_pairs={{0,1},{1,0},{2,3},{3,2},{4,5},{5,4},{6,7},{7,6},{8,9},{9,8},{10,11... | collective-permute-start | bytes 1572872 | tf_op jit(solution)/shard_map/ppermute | solution.py:259
  63.5 0.8 copy-start.2
  70.7 2.2 %collective-permute-start.3 = (bf16[2,128,896]{2,1,0:T(8,128)(2,1)}, bf16[2,128,896]{2,1,0:T(8,128)(2,1)S(1)}, u32[]{:S(2)}, u32[]{:S(2)}) collective-permute-start(bf16[2,128,896]{2,1,0:T(8,128)(2,1)} %get-tuple-element.8), channel_id=1, source_target_pairs={{0,1},{1,0},{2,3},{3,2},{4,5},{5,4},{6,7},{7,6},{8,9},{9,8},{10,11... | collective-permute-start | bytes 1376264 | tf_op jit(solution)/shard_map/ppermute | solution.py:259
  74.8 18.0 %all-to-all-start.2 = ((bf16[16,16,896]{2,1,0:T(8,128)(2,1)}), bf16[16,16,896]{2,1,0:T(8,128)(2,1)S(1)}, u32[]{:S(2)}, u32[]{:S(2)}) async-start(bf16[16,16,896]{2,1,0:T(8,128)(2,1)} %bitcast.16), calls=%async_computation.2 | async-start | bytes 917504 | tf_op jit(solution)/shard_map/all_to_all | solution.py:344

commit v3 on v2

v3 whole, which is shorter than its diff:
```python
import functools

import jax
import jax.numpy as jnp
from jax import lax
from jax.experimental import pallas as pl
from jax.experimental.pallas import tpu as pltpu
from jax.sharding import Mesh, PartitionSpec as P

TOPK = 8
SLOT_DEV = 2
CAP = 2
HOT = 2
CORES = 2
LANES = 128

score_scale = 192.0 ** (-0.5)
route_scale = 2.5
norm_eps = 1e-06
bf16 = jnp.bfloat16
f32 = jnp.float32


def keep_codes(token_experts, replica_pick, hot_experts, replica_index, experts):
    ids = lax.iota(jnp.int32, experts)
    held = jnp.where(
        replica_index[:, None] == lax.iota(jnp.int32, HOT)[None, :], hot_experts[None, :], 0
    ).sum(axis=1)
    count = 1 + jnp.sum((held[:, None] == ids[None, :]).astype(jnp.int32), axis=0)
    match = token_experts[:, :, None] == ids[None, None, :]
    named = jnp.any(match, axis=1)
    place = jnp.sum(jnp.where(match, replica_pick[:, :, None], 0), axis=1) % count[None, :]
    place = jnp.where(named, place, -1)
    tokens = lax.iota(jnp.int32, place.shape[0])
    ahead = (tokens[None, :] < tokens[:, None])[:, :, None] & (
        place[None, :, :] == place[:, None, :]
    )
    prior = jnp.sum(ahead.astype(jnp.int32), axis=1)
    return jnp.where(named, jnp.where(prior < CAP, 2.0, 1.0), 0.0)


def attend_kernel(
    steps, sub, block, lengths, ql, qr, cl, cr, residual, vu_hbm, out, lat, vu, wide_res, sem
):
    step = pl.program_id(0)
    per, heads = ql.shape[:2]
    here = per * steps
    tp = lax.axis_index("y") * lax.axis_size("c") + lax.axis_index("c")
    copy = pltpu.make_async_copy(vu_hbm, vu, sem)
    vdim = vu.shape[2]
    values = heads * vdim

    @pl.when(step == 0)
    def _():
        copy.start()
        width = residual.shape[1]
        wide_res[...] = residual[...].astype(f32)
        span = 2 * LANES
        lane = lax.broadcasted_iota(jnp.int32, (here, LANES), 1)
        for j in range(out.shape[0]):
            base = j * block + tp * sub
            start = jnp.minimum(base // LANES * LANES, width - span)
            piece = wide_res[:, pl.ds(pl.multiple_of(start, LANES), span)]
            piece = pltpu.roll(piece, span - (base - start), axis=1)[:, :LANES]
            out[j, :, values:] = jnp.where(lane < sub, piece, 0.0).astype(bf16)

    scores = [
        lax.dot_general(ql[i], cl[i], (((1,), (1,)), ((), ())), preferred_element_type=f32)
        for i in range(per)
    ]
    scores = [
        (s + jnp.dot(qr[i], cr[i], preferred_element_type=f32)) * score_scale
        for i, s in enumerate(scores)
    ]
    places = lax.broadcasted_iota(jnp.int32, scores[0].shape, 1)
    scores = [
        jnp.where(places < lengths[step * per + i], s, -1e30) for i, s in enumerate(scores)
    ]
    peaks = [jnp.max(s, axis=1, keepdims=True) for s in scores]
    shifted = [jnp.exp(s - m) for s, m in zip(scores, peaks)]
    inverse = [1.0 / jnp.sum(p, axis=1, keepdims=True) for p in shifted]
    mixed = [
        jnp.dot(p.astype(bf16), cl[i], preferred_element_type=f32)
        for i, p in enumerate(shifted)
    ]
    for i in range(per):
        got = mixed[i] * inverse[i]
        for j in range(lat.shape[0]):
            lat[j, pl.ds((step * per + i) * heads, heads), :] = got[
                :, j * LANES : (j + 1) * LANES
            ]

    @pl.when(step == steps - 1)
    def _():
        copy.wait()
        head_rows = lambda h: jnp.concatenate(
            [lat[j, pl.ds(h, here, stride=heads), :] for j in range(lat.shape[0])], axis=1
        ).astype(bf16)
        for h in range(0, heads, 2):
            rows = jnp.concatenate([head_rows(h), head_rows(h + 1)], axis=0)
            both = jnp.concatenate([vu[h], vu[h + 1]], axis=1)
            got = jnp.dot(rows, both, preferred_element_type=f32).astype(bf16)
            for j in range(out.shape[0]):
                out[j, :, h * vdim : (h + 1) * vdim] = got[:here, :vdim]
                out[j, :, (h + 1) * vdim : (h + 2) * vdim] = got[here:, vdim:]


def attend(
    query_latent, query_rope, cache_latent, cache_rope, lengths, value_up, residual, dests, sub, block
):
    here, heads, latent = query_latent.shape
    rope, places = cache_rope.shape[1:]
    vdim = value_up.shape[2]
    steps = 4
    per = here // steps
    spec = lambda *dims: pl.BlockSpec((per,) + dims, lambda t: (t,) + (0,) * len(dims))
    whole = lambda shape: pl.BlockSpec(shape, lambda t: (0,) * len(shape))
    out_shape = (dests, here, heads * vdim + LANES)
    return pl.pallas_call(
        functools.partial(attend_kernel, steps, sub, block),
        grid=(steps,),
        out_shape=jax.ShapeDtypeStruct(out_shape, bf16),
        in_specs=[
            pl.BlockSpec(memory_space=pltpu.SMEM),
            spec(heads, latent),
            spec(heads, rope),
            spec(places, latent),
            spec(rope, places),
            whole(residual.shape),
            pl.BlockSpec(memory_space=pl.ANY),
        ],
        out_specs=whole(out_shape),
        scratch_shapes=[
            pltpu.VMEM((latent // LANES, here * heads, LANES), f32),
            pltpu.VMEM(value_up.shape, bf16),
            pltpu.VMEM(residual.shape, f32),
            pltpu.SemaphoreType.DMA,
        ],
        compiler_params=pltpu.CompilerParams(
            dimension_semantics=("arbitrary",), vmem_limit_bytes=24 * 2**20
        ),
        name="attend",
    )(lengths, query_latent, query_rope, cache_latent, cache_rope, residual, value_up)


def expert_kernel(dims, mine, other, gate, up, down, keep_out, send_out, extras):
    n_ep, n_y, quarter, block, experts, part = dims
    core, ep = lax.axis_index("c"), lax.axis_index("ep")
    half = n_y * quarter
    here = 2 * half // n_ep
    per_quarter = quarter // here
    spare = mine.shape[3] - block

    lane = lax.broadcasted_iota(jnp.int32, (half, LANES), 1)
    sums = []
    sides = []
    for src in (mine, other):
        pieces = []
        total = jnp.zeros((half, LANES), f32)
        for j in range(0, n_ep, 2):
            low = src[:, j].reshape(half, -1)
            high = src[:, j + 1].reshape(half, -1)
            shared = jnp.where(lane < spare, low[:, -LANES:], high[:, :LANES])
            pieces += [low[:, :-LANES], shared, high[:, LANES:]]
            total += jnp.where(
                lane < spare, high[:, :LANES].astype(f32), low[:, -LANES:].astype(f32)
            )
        sides.append(jnp.concatenate(pieces, axis=1))
        sums.append(total)
    x = jnp.concatenate(sides, axis=0)
    total = jnp.concatenate(sums, axis=0)
    total = total[:, :spare] + total[:, spare:]
    for j in range(n_ep):
        y_of, rest = j // (per_quarter * 2), j % (per_quarter * 2)
        core_of, slot = rest // per_quarter, rest % per_quarter
        at = jnp.where(core == core_of, 0, half) + y_of * quarter + slot * here
        own = mine[0, j, :here, :]
        own = own[:, :spare] if j % 2 else own[:, block:]
        extras[pl.ds(pl.multiple_of(at, here), here), :] = own.astype(f32)
    square, logits, code = spare_lanes(total, extras[...], experts)

    gate_val = jnp.dot(x, gate[...], preferred_element_type=f32)
    up_val = jnp.dot(x, up[...], preferred_element_type=f32)
    scale = lax.rsqrt(square / (n_ep * block) + norm_eps)
    weight = row_weight(logits * scale, code, ep)
    act = (jax.nn.silu(gate_val * scale) * (up_val * (scale * weight))).astype(bf16)
    for flip, out in ((1, send_out), (0, keep_out)):
        to_core = jnp.where(core == 0, flip, 1 - flip)
        for y in range(n_y):
            cols = pl.ds(pl.multiple_of((y * 2 + to_core) * part, LANES), part)
            got = jnp.dot(act, down[:, cols], preferred_element_type=f32).astype(bf16)
            for i in range(2):
                of_core = jnp.where(core == 0, i, 1 - i)
                for q in range(n_y):
                    at = pl.multiple_of((q * 2 + of_core) * quarter, quarter)
                    src = i * half + q * quarter
                    out[y, pl.ds(at, quarter), :] = got[src : src + quarter, :]


def spare_lanes(total, own, experts):
    square = total[:, 0:1] + total[:, 1:2]
    logits = total[:, 2 : 2 + experts] + total[:, 2 + experts : 2 + 2 * experts]
    return square, logits, own[:, 2 + 2 * experts : 2 + 3 * experts]


def row_weight(logits, code, ep):
    affinity = jnp.where(code > 0.5, jax.nn.sigmoid(logits), 0.0)
    gates = route_scale * affinity / jnp.sum(affinity, axis=1, keepdims=True)
    mine_only = lax.broadcasted_iota(jnp.int32, gates.shape, 1) == ep
    return jnp.sum(jnp.where(mine_only & (code > 1.5), gates, 0.0), axis=1, keepdims=True)


def expert_block(mine, other, gate, up, down, block, experts):
    n_y, n_ep, quarter, wide = mine.shape
    tokens = 2 * n_y * quarter
    part = down.shape[1] // (2 * n_y)
    dims = (n_ep, n_y, quarter, block, experts, part)
    vmem = pl.BlockSpec(memory_space=pltpu.VMEM)
    shape = jax.ShapeDtypeStruct((n_y, tokens, part), bf16)
    return pl.pallas_call(
        functools.partial(expert_kernel, dims),
        out_shape=(shape, shape),
        in_specs=[vmem] * 5,
        out_specs=(vmem, vmem),
        scratch_shapes=[pltpu.VMEM((tokens, wide - block), f32)],
        compiler_params=pltpu.CompilerParams(vmem_limit_bytes=24 * 2**20),
        name="experts",
    )(mine, other, gate, up, down)


def expert_plain(ep, c, mine, other, gate, up, down, block, experts):
    n_y, n_ep, quarter, _ = mine.shape
    tokens = 2 * n_y * quarter
    here = tokens // n_ep
    part = down.shape[1] // (2 * n_y)
    both = jnp.stack([jnp.where(c == 0, mine, other), jnp.where(c == 0, other, mine)], axis=1)
    own = both[0, 0, :, :here, block:].reshape(tokens, -1).astype(f32)
    total = jnp.sum(both[..., block:].astype(f32), axis=2).reshape(tokens, -1)
    square, logits, code = spare_lanes(total, own, experts)
    x = both[..., :block].transpose(0, 1, 3, 2, 4).reshape(tokens, -1)
    scale = lax.rsqrt(square / x.shape[1] + norm_eps)
    weight = row_weight(logits * scale, code, ep)
    gate_val = jnp.dot(x, gate, preferred_element_type=f32) * scale
    up_val = jnp.dot(x, up, preferred_element_type=f32) * scale
    act = (jax.nn.silu(gate_val) * up_val * weight).astype(bf16)
    partial = jnp.dot(act, down, preferred_element_type=f32).astype(bf16)
    split = partial.reshape(tokens, n_y, 2, part).transpose(2, 1, 0, 3)
    return (
        lax.dynamic_index_in_dim(split, c, 0, keepdims=False),
        lax.dynamic_index_in_dim(split, 1 - c, 0, keepdims=False),
    )


def exchange(block, axis, size, mine):
    pieces = []
    for k in range(1, size):
        sent = lax.dynamic_index_in_dim(block, mine ^ k, 0, keepdims=False)
        pieces.append(lax.ppermute(sent, axis, [(i, i ^ k) for i in range(size)]))
    return lax.dynamic_index_in_dim(block, mine, 0, keepdims=False), pieces


def high_low(value):
    high = lax.reduce_precision(value, 8, 7)
    return [high.astype(bf16), (value - high).astype(bf16)]


def swap_cores(block):
    return lax.ppermute(block, "c", [(0, 1), (1, 0)])


def per_device(
    query_latent,
    query_rope,
    cache_latent,
    cache_rope,
    cache_lengths,
    value_up,
    out_proj,
    residual,
    norm_gain,
    router,
    trainer_gate,
    trainer_up,
    trainer_down,
    hot_experts,
    replica_index,
    token_experts,
    replica_pick,
):
    n_ep, n_y, n_c = lax.axis_size("ep"), lax.axis_size("y"), lax.axis_size("c")
    n_tp = n_y * n_c
    ep, y, c = lax.axis_index("ep"), lax.axis_index("y"), lax.axis_index("c")
    tp = y * n_c + c
    here, width = residual.shape
    tokens = here * n_ep
    quarter = tokens // n_tp
    experts = router.shape[1]
    block = out_proj.shape[0]
    sub = block // n_tp
    part = width // n_tp

    parcel = attend(
        query_latent, query_rope, cache_latent, cache_rope, cache_lengths, value_up,
        residual, n_ep, sub, block,
    )
    sub_wide = LANES
    inner = parcel.shape[2] - sub_wide
    landed = lax.all_to_all(parcel, "ep", split_axis=0, concat_axis=0, tiled=True)
    landed = landed.reshape(tokens, -1)
    at_row = lax.broadcasted_iota(jnp.int32, (sub_wide, block), 0)
    at_col = lax.broadcasted_iota(jnp.int32, (sub_wide, block), 1)
    spot = ((at_row + tp * sub == at_col) & (at_row < sub)).astype(bf16)
    column_part = lax.dot_general(
        landed[:, :inner], out_proj, (((1,), (1,)), ((), ())), preferred_element_type=f32
    ) + jnp.dot(landed[:, inner:], spot, preferred_element_type=f32)

    halves = column_part.reshape(n_y, n_c, quarter, block).transpose(1, 0, 2, 3)
    own, others = exchange(halves, "c", n_c, c)
    half = own + sum(others)
    own, others = exchange(half, "y", n_y, y)
    hidden_part = own + sum(others)

    codes = keep_codes(token_experts, replica_pick, hot_experts, replica_index, experts)
    codes = jnp.pad(codes.astype(bf16), ((0, quarter - here), (0, 0)))
    gain_part = lax.dynamic_slice_in_dim(norm_gain, ep * block, block, 0)
    router_part = lax.dynamic_slice_in_dim(router, ep * block, block, 0)
    scaled = (hidden_part * gain_part[None, :]).astype(bf16)
    square = jnp.sum(hidden_part * hidden_part, axis=1, keepdims=True)
    logits = jnp.dot(scaled, router_part, preferred_element_type=f32)
    wide = -(-(block + 2 + 3 * experts) // LANES) * LANES
    extras = jnp.concatenate(
        high_low(square)
        + high_low(logits)
        + [codes, jnp.zeros((quarter, wide - block - 2 - 3 * experts), bf16)],
        axis=1,
    )
    paired = block % LANES == LANES // 2 == wide - block and n_ep // n_tp % 2 == 0
    sent = jnp.concatenate([scaled, extras], axis=1)
    if paired:
        sent = jnp.where(ep % 2 == 0, sent, jnp.concatenate([extras, scaled], axis=1))
    count = n_y * n_ep
    mine = lax.all_to_all(
        jnp.broadcast_to(sent[None], (count, quarter, wide)),
        ("y", "ep"),
        split_axis=0,
        concat_axis=0,
        tiled=True,
    ).reshape(n_y, n_ep, quarter, wide)
    other = swap_cores(mine)

    weights = (trainer_gate[0], trainer_up[0], trainer_down[0])
    if paired and block % 16 == 0 and tokens <= 256:
        keep, send = expert_block(mine, other, *weights, block, experts)
    else:
        keep, send = expert_plain(ep, c, mine, other, *weights, block, experts)

    got = swap_cores(send)
    summed = (keep.astype(f32) + got.astype(f32)).astype(bf16)
    outbound = summed.reshape(count, here, part)
    returned = lax.all_to_all(outbound, ("y", "ep"), split_axis=0, concat_axis=0, tiled=True)
    moe = jnp.sum(returned.astype(f32), axis=0)

    per_part = n_ep // n_tp
    first = ep * here
    of_tp, row = first // quarter, first % quarter
    cut = lambda a: lax.dynamic_slice(
        a, (of_tp // n_c, tp * per_part, row, 0), (1, per_part, here, wide)
    )[0]
    rows = jnp.where(of_tp % n_c == c, cut(mine), cut(other))
    pieces = [
        rows[j, :, wide - block :] if paired and j % 2 else rows[j, :, :block]
        for j in range(per_part)
    ]
    gain_own = lax.dynamic_slice_in_dim(norm_gain, tp * part, part, 0)
    hidden_own = jnp.concatenate(pieces, axis=1).astype(f32) / gain_own[None, :]
    return (hidden_own + moe).astype(bf16)


def solution(mesh):
    n_ep, n_tp = mesh.shape["ep"], mesh.shape["tp"]
    fine = Mesh(mesh.devices.reshape(n_ep, n_tp // CORES, CORES), ("ep", "y", "c"))
    tp = ("y", "c")
    placed = (
        P("ep", tp, None),
        P("ep", tp, None),
        P("ep", None, None),
        P("ep", None, None),
        P("ep"),
        P(tp, None, None),
        P("ep", tp),
        P("ep", None),
        P(),
        P(),
        P("ep", None, tp),
        P("ep", None, tp),
        P("ep", tp, None),
        P(),
        P(),
        P("ep", None),
        P("ep", None),
    )
    return jax.shard_map(
        per_device, mesh=fine, in_specs=placed, out_specs=P("ep", tp), check_vma=False
    )
```

time: 94 us -> 92.8 us (0.987)
  Pallas kernels: 17.1 us -> 5.93 us
  local copies, waits for them, and re-layouts: 5.32 us -> 15.5 us
  other arithmetic: 4.93 us -> 2.63 us
  waiting for transfers between devices: 33 us -> 34.4 us
    unnamed x21 -> x31, local copies, waits for them, and re-layouts: 2.17 us -> 12.9 us
    pallas_call x1, Pallas kernels: 10.6 us -> 4.78 us  [attend(): pl.pallas_call(functools.partial(attend_kernel, steps, sub, block), grid=...]
    pallas_call x1, Pallas kernels: 6.44 us -> 1.15 us  [expert_block(): pl.pallas_call(functools.partial(expert_kernel, dims), out_shape=(shape,...]
    ppermute x2, waiting for transfers between devices: 1.66 us -> 3.59 us  [swap_cores(): return lax.ppermute(block, 'c', [(0, 1), (1, 0)])]
    dynamic_slice x1 -> x2, local copies, waits for them, and re-layouts: 0.08 us -> 1.55 us  [the longest x1 0.78 us: per_device(): gain_own = lax.dynamic_slice_in_dim(norm_gain, tp * part, part, 0)]
    reshape x1 -> x0, local copies, waits for them, and re-layouts: 1.23 us -> none  [per_device(): shares = residual.reshape(here, n_ep, n_tp, sub)]
    convert_element_type x1, other arithmetic: 1.89 us -> 0.87 us  [per_device(): summed = (keep.astype(f32) + got.astype(f32)).astype(bf16)]
  transfers between devices with their start and end apart: 6 -> 6, of which waited for: 5 -> 6; matrix products, arithmetic and copies ran while one was open for 5% -> 3% of each run, Pallas kernels for 0% -> 0%
where the time goes in v3:
time: 92.8 us; the launch traced here: 92.1 us
  waiting for transfers between devices  34.4 us (37%)
  blocking collectives  18.8 us (20%)
  local copies, waits for them, and re-layouts  15.5 us (17%)
  starting transfers between devices  12.7 us (14%)
  Pallas kernels  5.93 us (6%)
  other arithmetic  2.63 us (3%)
  matrix products  1.87 us (2%)
    all_to_all x1, blocking collectives, per_device(): lax.all_to_all(jnp.broadcast_to(sent[None], (count, quarter, wide)), ('y'...  18.8 us
    all_to_all x1, waiting for transfers between devices, per_device(): lax.all_to_all(parcel, 'ep', split_axis=0, concat_axis=0, tiled=True)  14.6 us
    all_to_all x1, waiting for transfers between devices, per_device(): lax.all_to_all(outbound, ('y', 'ep'), split_axis=0, concat_axis=0, tiled=...  13.4 us
    unnamed x31, local copies, waits for them, and re-layouts  12.9 us
    all_to_all x1, starting transfers between devices, per_device(): lax.all_to_all(parcel, 'ep', split_axis=0, concat_axis=0, tiled=True)  7.29 us
    pallas_call x1, Pallas kernels, attend(): pl.pallas_call(functools.partial(attend_kernel, steps, sub, block), grid=...  4.78 us
    ppermute x2, waiting for transfers between devices, swap_cores(): return lax.ppermute(block, 'c', [(0, 1), (1, 0)])  3.59 us
    all_to_all x1, starting transfers between devices, per_device(): lax.all_to_all(outbound, ('y', 'ep'), split_axis=0, concat_axis=0, tiled=...  3.59 us
  transfers between devices with their start and end apart: 6, of which 6 were waited for; matrix products, arithmetic and copies ran while one was open for 3% of the time, Pallas kernels for 0%

profile of v3, /device:TPU:0, one launch (start us, length us, event | category | flops | bytes accessed | tf_op | source)
XLA Modules:
  0.0 92.1 jit_solution(13897529995478650218)
XLA Ops:
  0.0 0.0 copy-start
  0.0 0.0 copy-start.1
  0.0 2.3 %copy-done.1 = bf16[16,256,512]{2,1,0:T(8,128)(2,1)S(1)} copy-done((bf16[16,256,512]{2,1,0:T(8,128)(2,1)S(1)}, bf16[16,256,512]{2,1,0:T(8,128)(2,1)}, u32[]{:S(2)}) %copy-start.1) | copy-done | bytes 4194328
  2.3 0.0 copy-start.2
  2.3 1.6 %copy-done.2 = bf16[16,512,128]{2,1,0:T(8,128)(2,1)S(1)} copy-done((bf16[16,512,128]{2,1,0:T(8,128)(2,1)S(1)}, bf16[16,512,128]{2,1,0:T(8,128)(2,1)}, u32[]{:S(2)}) %copy-start.2) | copy-done | bytes 2097176
  3.9 0.0 copy-start.6
  3.9 1.0 %copy-done.6 = bf16[16,64,256]{2,1,0:T(8,128)(2,1)S(1)} copy-done((bf16[16,64,256]{2,1,0:T(8,128)(2,1)S(1)}, bf16[16,64,256]{2,1,0:T(8,128)(2,1)}, u32[]{:S(2)}) %copy-start.6) | copy-done | bytes 524312
  5.0 0.0 copy-start.7
  5.0 0.9 %copy-done.7 = bf16[16,16,512]{2,1,0:T(8,128)(2,1)S(1)} copy-done((bf16[16,16,512]{2,1,0:T(8,128)(2,1)S(1)}, bf16[16,16,512]{2,1,0:T(8,128)(2,1)}, u32[]{:S(2)}) %copy-start.7) | copy-done | bytes 262168
  5.9 0.0 copy-start.8
  5.9 0.9 copy-done.8
  6.8 0.0 copy-start.9
  6.8 0.8 copy-done.9
  7.6 0.0 copy-start.10
  7.7 0.7 copy-done.10
  8.3 0.0 copy-start.13
  8.3 0.0 copy-start.14
  8.3 4.8 %attend.1 = bf16[8,16,2176]{2,1,0:T(8,128)(2,1)} custom-call(s32[16]{0:T(128)S(1)} %copy-done.10, bf16[16,16,512]{2,1,0:T(8,128)(2,1)S(1)} %copy-done.7, bf16[16,16,64]{2,1,0:T(8,128)(2,1)S(1)} %copy-done.9, bf16[16,256,512]{2,1,0:T(8,128)(2,1)S(1)} %copy-done.1, bf16[16,64,256]{2,1,0:T(8,128)(2,1)S(1)} %copy-done.6, bf16[16,3584]{1,0:T(8,128)(2,1)S(1)} %copy-done.8, ...), custom_call_target="tpu_custom_call" | custom-call | tf_op jit(solution)/shard_map/attend/pallas_call | solution.py:119
  13.1 7.3 %all-to-all-start = ((bf16[8,16,2176]{2,1,0:T(8,128)(2,1)}), bf16[8,16,2176]{2,1,0:T(8,128)(2,1)S(1)}, u32[]{:S(2)}, u32[]{:S(2)}) async-start(bf16[8,16,2176]{2,1,0:T(8,128)(2,1)} %attend.1), calls=%async_computation | async-start | bytes 1114112 | tf_op jit(solution)/shard_map/all_to_all | solution.py:308
  20.4 0.0 copy-done.13
  20.4 0.0 copy-done.14
  20.4 0.1 fusion.13
  20.5 0.1 convert_reduce_fusion.2
  20.6 0.0 copy-done.11
  20.6 0.0 copy-done.12
  20.7 0.2 fusion.11
  20.8 0.1 copy.42
  20.9 14.6 %all-to-all-done = bf16[8,16,2176]{2,1,0:T(8,128)(2,1)S(1)} async-done(((bf16[8,16,2176]{2,1,0:T(8,128)(2,1)}), bf16[8,16,2176]{2,1,0:T(8,128)(2,1)S(1)}, u32[]{:S(2)}, u32[]{:S(2)}) %all-to-all-start) | async-done | bytes 557088 | tf_op jit(solution)/shard_map/all_to_all | solution.py:308
  35.6 0.3 fusion.2
  35.9 0.0 copy-done
  35.9 0.6 convolution_add_fusion
  36.6 0.1 copy.41
  36.7 0.1 collective-permute-start
  36.8 0.4 convert_reduce_fusion.1
  37.2 0.1 copy.43
  37.3 0.8 collective-permute-done
  38.2 1.6 %collective-permute-start.1 = (f32[32,448]{1,0:T(8,128)S(1)}, f32[32,448]{1,0:T(8,128)S(1)}, u32[]{:S(2)}, u32[]{:S(2)}) collective-permute-start(f32[32,448]{1,0:T(8,128)S(1)} %dynamic-slice_bitcast_fusion.1), channel_id=1, source_target_pairs={{0,2},{2,0},{1,3},{3,1},{4,6},{6,4},{5,7},{7,5},{8,10},{10,8},{9,1... | collective-permute-start | bytes 172040 | tf_op jit(solution)/shard_map/ppermute | solution.py:258
  39.8 0.1 copy.54
  39.9 0.8 dynamic_slice.27
  40.6 1.9 %collective-permute-done.1 = f32[32,448]{1,0:T(8,128)S(1)} collective-permute-done((f32[32,448]{1,0:T(8,128)S(1)}, f32[32,448]{1,0:T(8,128)S(1)}, u32[]{:S(2)}, u32[]{:S(2)}) %collective-permute-start.1) | collective-permute-done | bytes 57376 | tf_op jit(solution)/shard_map/ppermute | solution.py:258
  42.5 0.1 multiply_reduce_fusion
  42.6 0.9 fusion.10
  43.5 0.1 copy.46
  43.6 0.1 copy.47
  43.7 0.1 copy.44
  43.8 0.1 copy.45
  43.9 0.1 concatenate.21
  44.1 0.1 concatenate.20
  44.2 18.8 %all_to_all.15 = bf16[16,32,512]{2,1,0:T(8,128)(2,1)S(1)} all-to-all(bf16[16,32,512]{2,1,0:T(8,128)(2,1)S(1)} %broadcast_in_dim.75), channel_id=1, replica_groups=mesh['ep'=8,'y'=2,'c'=2] {'y','ep'}, dimensions={0} | all-to-all | bytes 1048576 | tf_op jit(solution)/shard_map/all_to_all | solution.py:342
  63.0 0.0 collective-permute-start.2
  63.0 1.9 %collective-permute-done.2.other = bf16[2,8,32,512]{3,2,1,0:T(8,128)(2,1)S(1)} collective-permute-done((bf16[2,8,32,512]{3,2,1,0:T(8,128)(2,1)S(1)}, bf16[2,8,32,512]{3,2,1,0:T(8,128)(2,1)S(1)}, u32[]{:S(2)}, u32[]{:S(2)}) %collective-permute-start.2) | collective-permute-done | bytes 524320 | tf_op jit(solution)/shard_map/ppermute | solution.py:268
  64.9 1.5 %copy-done.3 = bf16[1,3584,256]{2,1,0:T(8,128)(2,1)S(1)} copy-done((bf16[1,3584,256]{2,1,0:T(8,128)(2,1)S(1)}, bf16[1,3584,256]{2,1,0:T(8,128)(2,1)}, u32[]{:S(2)}) %copy-start.3) | copy-done | bytes 1835032
  66.4 1.5 %copy-done.4 = bf16[1,3584,256]{2,1,0:T(8,128)(2,1)S(1)} copy-done((bf16[1,3584,256]{2,1,0:T(8,128)(2,1)S(1)}, bf16[1,3584,256]{2,1,0:T(8,128)(2,1)}, u32[]{:S(2)}) %copy-start.4) | copy-done | bytes 1835032
  67.9 1.5 %copy-done.5 = bf16[1,256,3584]{2,1,0:T(8,128)(2,1)S(1)} copy-done((bf16[1,256,3584]{2,1,0:T(8,128)(2,1)S(1)}, bf16[1,256,3584]{2,1,0:T(8,128)(2,1)}, u32[]{:S(2)}) %copy-start.5) | copy-done | bytes 1835032
  69.4 1.2 %experts.1 = (bf16[2,128,896]{2,1,0:T(8,128)(2,1)S(1)}, bf16[2,128,896]{2,1,0:T(8,128)(2,1)S(1)}) custom-call(bf16[2,8,32,512]{3,2,1,0:T(8,128)(2,1)S(1)} %bitcast.31, bf16[2,8,32,512]{3,2,1,0:T(8,128)(2,1)S(1)} %collective-permute-done.2.other, bf16[3584,256]{1,0:T(8,128)(2,1)S(1)} %bitcast.33, bf16[3584,256]{1,0:T(8,128)(2,1)S(1)} %bitcast.34, ...), custom_call_target="tpu_custom_call" | custom-call | tf_op jit(solution)/shard_map/experts/pallas_call | solution.py:220
  70.6 0.2 collective-permute-start.3
  70.8 1.7 %collective-permute-done.3 = bf16[2,128,896]{2,1,0:T(8,128)(2,1)S(1)} collective-permute-done((bf16[2,128,896]{2,1,0:T(8,128)(2,1)S(1)}, bf16[2,128,896]{2,1,0:T(8,128)(2,1)S(1)}, u32[]{:S(2)}, u32[]{:S(2)}) %collective-permute-start.3) | collective-permute-done | bytes 458784 | tf_op jit(solution)/shard_map/ppermute | solution.py:268
  72.5 0.9 add_convert_fusion
  73.3 3.6 %all-to-all-start.2 = ((bf16[16,16,896]{2,1,0:T(8,128)(2,1)}), bf16[16,16,896]{2,1,0:T(8,128)(2,1)S(1)}, u32[]{:S(2)}, u32[]{:S(2)}) async-start(bf16[16,16,896]{2,1,0:T(8,128)(2,1)} %bitcast.38), calls=%async_computation.2 | async-start | bytes 917504 | tf_op jit(solution)/shard_map/all_to_all | solution.py:360
  77.0 0.8 dynamic_slice.31
  77.8 0.1 slice_bitcast_fusion.1
  77.9 13.4 %all-to-all-done.2 = bf16[16,16,896]{2,1,0:T(8,128)(2,1)S(1)} async-done(((bf16[16,16,896]{2,1,0:T(8,128)(2,1)}), bf16[16,16,896]{2,1,0:T(8,128)(2,1)S(1)}, u32[]{:S(2)}, u32[]{:S(2)}) %all-to-all-start.2) | async-done | bytes 458784 | tf_op jit(solution)/shard_map/all_to_all | solution.py:360
  91.3 0.1 convert_reduce_fusion
  91.4 0.7 add_convert_fusion.1
  (22 shorter events, 0.2 us)
Async XLA Ops:
  0.0 35.9 %copy-start = (bf16[448,2048]{1,0:T(8,128)(2,1)S(1)}, bf16[448,2048]{1,0:T(8,128)(2,1)}, u32[]{:S(2)}) copy-start(bf16[448,2048]{1,0:T(8,128)(2,1)} %param.23) | copy-start | bytes 5505028
  0.0 2.3 %copy-start.1 = (bf16[16,256,512]{2,1,0:T(8,128)(2,1)S(1)}, bf16[16,256,512]{2,1,0:T(8,128)(2,1)}, u32[]{:S(2)}) copy-start(bf16[16,256,512]{2,1,0:T(8,128)(2,1)} %cl.1) | copy-start | bytes 12582916
  2.3 1.6 %copy-start.2 = (bf16[16,512,128]{2,1,0:T(8,128)(2,1)S(1)}, bf16[16,512,128]{2,1,0:T(8,128)(2,1)}, u32[]{:S(2)}) copy-start(bf16[16,512,128]{2,1,0:T(8,128)(2,1)} %vu_hbm.1) | copy-start | bytes 6291460
  3.9 1.0 %copy-start.6 = (bf16[16,64,256]{2,1,0:T(8,128)(2,1)S(1)}, bf16[16,64,256]{2,1,0:T(8,128)(2,1)}, u32[]{:S(2)}) copy-start(bf16[16,64,256]{2,1,0:T(8,128)(2,1)} %cr.1) | copy-start | bytes 1572868
  5.0 0.9 %copy-start.7 = (bf16[16,16,512]{2,1,0:T(8,128)(2,1)S(1)}, bf16[16,16,512]{2,1,0:T(8,128)(2,1)}, u32[]{:S(2)}) copy-start(bf16[16,16,512]{2,1,0:T(8,128)(2,1)} %ql.1) | copy-start | bytes 786436
  5.9 0.9 copy-start.8
  6.8 0.8 copy-start.9
  7.6 0.7 copy-start.10
  8.3 12.1 %copy-start.13 = (s32[2]{0:T(128)S(1)}, s32[2]{0:T(128)}, u32[]{:S(2)}) copy-start(s32[2]{0:T(128)} %param.30) | copy-start | bytes 28
  8.3 12.1 %copy-start.14 = (s32[8]{0:T(128)S(1)}, s32[8]{0:T(128)}, u32[]{:S(2)}) copy-start(s32[8]{0:T(128)} %param.31) | copy-start | bytes 100
  8.3 12.3 %copy-start.11 = (s32[16,8]{0,1:T(8,128)S(1)}, s32[16,8]{0,1:T(8,128)}, u32[]{:S(2)}) copy-start(s32[16,8]{0,1:T(8,128)} %param.32) | copy-start | bytes 1540
  8.3 12.3 %copy-start.12 = (s32[16,8]{0,1:T(8,128)S(1)}, s32[16,8]{0,1:T(8,128)}, u32[]{:S(2)}) copy-start(s32[16,8]{0,1:T(8,128)} %param.33) | copy-start | bytes 1540
  13.1 22.5 %all-to-all-start = ((bf16[8,16,2176]{2,1,0:T(8,128)(2,1)}), bf16[8,16,2176]{2,1,0:T(8,128)(2,1)S(1)}, u32[]{:S(2)}, u32[]{:S(2)}) async-start(bf16[8,16,2176]{2,1,0:T(8,128)(2,1)} %attend.1), calls=%async_computation | async-start | bytes 1114112 | tf_op jit(solution)/shard_map/all_to_all | solution.py:308
  36.7 1.4 %collective-permute-start = (f32[2,32,448]{2,1,0:T(8,128)S(1)}, f32[2,32,448]{2,1,0:T(8,128)S(1)}, u32[]{:S(2)}, u32[]{:S(2)}) collective-permute-start(f32[2,32,448]{2,1,0:T(8,128)S(1)} %dynamic-slice_bitcast_fusion), channel_id=1, source_target_pairs={{0,1},{1,0},{2,3},{3,2},{4,5},{5,4},{6,7},{7,6},{8,9},{9,8},{10,11... | collective-permute-start | bytes 344072 | tf_op jit(solution)/shard_map/ppermute | solution.py:258
  38.2 4.3 %collective-permute-start.1 = (f32[32,448]{1,0:T(8,128)S(1)}, f32[32,448]{1,0:T(8,128)S(1)}, u32[]{:S(2)}, u32[]{:S(2)}) collective-permute-start(f32[32,448]{1,0:T(8,128)S(1)} %dynamic-slice_bitcast_fusion.1), channel_id=1, source_target_pairs={{0,2},{2,0},{1,3},{3,1},{4,6},{6,4},{5,7},{7,5},{8,10},{10,8},{9,1... | collective-permute-start | bytes 172040 | tf_op jit(solution)/shard_map/ppermute | solution.py:258
  63.0 1.9 %collective-permute-start.2 = (bf16[2,8,32,512]{3,2,1,0:T(8,128)(2,1)S(1)}, bf16[2,8,32,512]{3,2,1,0:T(8,128)(2,1)S(1)}, u32[]{:S(2)}, u32[]{:S(2)}) collective-permute-start(bf16[2,8,32,512]{3,2,1,0:T(8,128)(2,1)S(1)} %bitcast.30), channel_id=1, source_target_pairs={{0,1},{1,0},{2,3},{3,2},{4,5},{5,4},{6,7},{7,6},{8,9},{9,8},{10,11... | collective-permute-start | bytes 1572872 | tf_op jit(solution)/shard_map/ppermute | solution.py:268
  64.9 1.5 %copy-start.3 = (bf16[1,3584,256]{2,1,0:T(8,128)(2,1)S(1)}, bf16[1,3584,256]{2,1,0:T(8,128)(2,1)}, u32[]{:S(2)}) copy-start(bf16[1,3584,256]{2,1,0:T(8,128)(2,1)} %param.27) | copy-start | bytes 5505028
  66.4 1.5 %copy-start.4 = (bf16[1,3584,256]{2,1,0:T(8,128)(2,1)S(1)}, bf16[1,3584,256]{2,1,0:T(8,128)(2,1)}, u32[]{:S(2)}) copy-start(bf16[1,3584,256]{2,1,0:T(8,128)(2,1)} %param.28) | copy-start | bytes 5505028
  67.9 1.5 %copy-start.5 = (bf16[1,256,3584]{2,1,0:T(8,128)(2,1)S(1)}, bf16[1,256,3584]{2,1,0:T(8,128)(2,1)}, u32[]{:S(2)}) copy-start(bf16[1,256,3584]{2,1,0:T(8,128)(2,1)} %param.29) | copy-start | bytes 5505028
  70.6 1.9 %collective-permute-start.3 = (bf16[2,128,896]{2,1,0:T(8,128)(2,1)S(1)}, bf16[2,128,896]{2,1,0:T(8,128)(2,1)S(1)}, u32[]{:S(2)}, u32[]{:S(2)}) collective-permute-start(bf16[2,128,896]{2,1,0:T(8,128)(2,1)S(1)} %get-tuple-element.8), channel_id=1, source_target_pairs={{0,1},{1,0},{2,3},{3,2},{4,5},{5,4},{6,7},{7,6},{8,9},{9,8},{10,11... | collective-permute-start | bytes 1376264 | tf_op jit(solution)/shard_map/ppermute | solution.py:268
  73.3 18.0 %all-to-all-start.2 = ((bf16[16,16,896]{2,1,0:T(8,128)(2,1)}), bf16[16,16,896]{2,1,0:T(8,128)(2,1)S(1)}, u32[]{:S(2)}, u32[]{:S(2)}) async-start(bf16[16,16,896]{2,1,0:T(8,128)(2,1)} %bitcast.38), calls=%async_computation.2 | async-start | bytes 917504 | tf_op jit(solution)/shard_map/all_to_all | solution.py:360

commit v4 on v3

--- a/solution.py
+++ b/solution.py
@@ -103,6 +103,113 @@
             for j in range(out.shape[0]):
                 out[j, :, h * vdim : (h + 1) * vdim] = got[:here, :vdim]
                 out[j, :, (h + 1) * vdim : (h + 2) * vdim] = got[here:, vdim:]
+
+
+def in_hbm(array):
+    return pltpu.with_memory_space_constraint(array, pltpu.HBM)
+
+
+def fetch_kernel(count, *refs):
+    sems = refs[-1]
+    ins, outs = refs[:count], refs[count : 2 * count]
+    copies = [pltpu.make_async_copy(a, b, sems.at[i]) for i, (a, b) in enumerate(zip(ins, outs))]
+    for copy in copies:
+        copy.start()
+    for copy in copies:
+        copy.wait()
+
+
+def fetch(*arrays):
+    count = len(arrays)
+    return pl.pallas_call(
+        functools.partial(fetch_kernel, count),
+        out_shape=tuple(jax.ShapeDtypeStruct(a.shape, a.dtype) for a in arrays),
+        in_specs=[pl.BlockSpec(memory_space=pl.ANY)] * count,
+        out_specs=(pl.BlockSpec(memory_space=pltpu.VMEM),) * count,
+        scratch_shapes=[pltpu.SemaphoreType.DMA((count,))],
+        compiler_params=pltpu.CompilerParams(vmem_limit_bytes=12 * 2**20),
+        cost_estimate=pl.CostEstimate(
+            flops=0, bytes_accessed=sum(2 * a.size * a.dtype.itemsize for a in arrays), transcendentals=0
+        ),
+        name="fetch",
+    )(*map(in_hbm, arrays))
+
+
+def project_kernel(sub, landed, out_proj, keep, send):
+    n_y, quarter, block = keep.shape
+    tokens = landed.shape[0]
+    inner = out_proj.shape[1]
+    core = lax.axis_index("c")
+    tp = lax.axis_index("y") * lax.axis_size("c") + core
+    rest = landed.shape[1] - inner
+    at_row = lax.broadcasted_iota(jnp.int32, (rest, block), 0)
+    at_col = lax.broadcasted_iota(jnp.int32, (rest, block), 1)
+    spot = jnp.where((at_row + tp * sub == at_col) & (at_row < sub), 1.0, 0.0).astype(bf16)
+    part = lax.dot_general(
+        landed[:, :inner], out_proj[...], (((1,), (1,)), ((), ())), preferred_element_type=f32
+    ) + jnp.dot(landed[:, inner:], spot, preferred_element_type=f32)
+    for y in range(n_y):
+        zero = part[2 * y * quarter : (2 * y + 1) * quarter]
+        one = part[(2 * y + 1) * quarter : (2 * y + 2) * quarter]
+        keep[y] = jnp.where(core == 0, zero, one)
+        send[y] = jnp.where(core == 0, one, zero)
+
+
+def project(landed, out_proj, sub, n_y):
+    tokens = landed.shape[0]
+    block = out_proj.shape[0]
+    vmem = pl.BlockSpec(memory_space=pltpu.VMEM)
+    shape = jax.ShapeDtypeStruct((n_y, tokens // (2 * n_y), block), f32)
+    return pl.pallas_call(
+        functools.partial(project_kernel, sub),
+        out_shape=(shape, shape),
+        in_specs=[vmem] * 2,
+        out_specs=(vmem, vmem),
+        compiler_params=pltpu.CompilerParams(vmem_limit_bytes=8 * 2**20),
+        name="project",
+    )(landed, out_proj)
+
+
+def bundle_kernel(own, got, gain, router_t, codes, out):
+    hidden = own[...] + got[...]
+    rows, block = hidden.shape
+    experts = router_t.shape[0]
+    scaled = (hidden * gain[...]).astype(bf16)
+    square = jnp.sum(hidden * hidden, axis=1, keepdims=True)
+    logits = lax.dot_general(
+        scaled, router_t[...], (((1,), (1,)), ((), ())), preferred_element_type=f32
+    )
+    spare = out.shape[2] - block
+    both = high_low(square) + high_low(logits) + [codes[...]]
+    extras = jnp.concatenate(
+        [b.astype(f32) for b in both] + [jnp.zeros((rows, spare - 2 - 3 * experts), f32)], axis=1
+    ).astype(bf16)
+    odd = lax.rem(lax.axis_index("ep"), 2) == 1
+
+    @pl.when(jnp.logical_not(odd))
+    def _():
+        row = jnp.concatenate([scaled, extras], axis=1)
+        for j in range(out.shape[0]):
+            out[j] = row
+
+    @pl.when(odd)
+    def _():
+        row = jnp.concatenate([extras, scaled], axis=1)
+        for j in range(out.shape[0]):
+            out[j] = row
+
+
+def bundle(own, got, gain, router_t, codes, count, wide):
+    rows = own.shape[0]
+    vmem = pl.BlockSpec(memory_space=pltpu.VMEM)
+    return pl.pallas_call(
+        bundle_kernel,
+        out_shape=jax.ShapeDtypeStruct((count, rows, wide), bf16),
+        in_specs=[vmem] * 5,
+        out_specs=vmem,
+        compiler_params=pltpu.CompilerParams(vmem_limit_bytes=4 * 2**20),
+        name="bundle",
+    )(own, got, gain, router_t, codes)
 
 
 def attend(
@@ -140,7 +247,7 @@
             dimension_semantics=("arbitrary",), vmem_limit_bytes=24 * 2**20
         ),
         name="attend",
-    )(lengths, query_latent, query_rope, cache_latent, cache_rope, residual, value_up)
+    )(lengths, *map(in_hbm, (query_latent, query_rope, cache_latent, cache_rope, residual, value_up)))
 
 
 def expert_kernel(dims, mine, other, gate, up, down, keep_out, send_out, extras):
@@ -261,7 +368,7 @@
 
 def high_low(value):
     high = lax.reduce_precision(value, 8, 7)
-    return [high.astype(bf16), (value - high).astype(bf16)]
+    return [high, value - high]
 
 
 def swap_cores(block):
@@ -307,50 +414,48 @@
     inner = parcel.shape[2] - sub_wide
     landed = lax.all_to_all(parcel, "ep", split_axis=0, concat_axis=0, tiled=True)
     landed = landed.reshape(tokens, -1)
-    at_row = lax.broadcasted_iota(jnp.int32, (sub_wide, block), 0)
-    at_col = lax.broadcasted_iota(jnp.int32, (sub_wide, block), 1)
-    spot = ((at_row + tp * sub == at_col) & (at_row < sub)).astype(bf16)
-    column_part = lax.dot_general(
-        landed[:, :inner], out_proj, (((1,), (1,)), ((), ())), preferred_element_type=f32
-    ) + jnp.dot(landed[:, inner:], spot, preferred_element_type=f32)
-
-    halves = column_part.reshape(n_y, n_c, quarter, block).transpose(1, 0, 2, 3)
-    own, others = exchange(halves, "c", n_c, c)
-    half = own + sum(others)
+    wide = -(-(block + 2 + 3 * experts) // LANES) * LANES
+    paired = block % LANES == LANES // 2 == wide - block and n_ep // n_tp % 2 == 0
+    paired = paired and block % 16 == 0 and tokens <= 256
+    weights = (trainer_gate[0], trainer_up[0], trainer_down[0])
+    gain_part = lax.dynamic_slice_in_dim(norm_gain, ep * block, block, 0)[None, :]
+    router_part = lax.dynamic_slice_in_dim(router.T, ep * block, block, 1)
+    if paired:
+        keep, send = project(landed, out_proj, sub, n_y)
+        half = keep + swap_cores(send)
+    else:
+        at_row = lax.broadcasted_iota(jnp.int32, (sub_wide, block), 0)
+        at_col = lax.broadcasted_iota(jnp.int32, (sub_wide, block), 1)
+        spot = ((at_row + tp * sub == at_col) & (at_row < sub)).astype(bf16)
+        column_part = lax.dot_general(
+            landed[:, :inner], out_proj, (((1,), (1,)), ((), ())), preferred_element_type=f32
+        ) + jnp.dot(landed[:, inner:], spot, preferred_element_type=f32)
+        halves = column_part.reshape(n_y, n_c, quarter, block).transpose(1, 0, 2, 3)
+        own, others = exchange(halves, "c", n_c, c)
+        half = own + sum(others)
     own, others = exchange(half, "y", n_y, y)
-    hidden_part = own + sum(others)
 
     codes = keep_codes(token_experts, replica_pick, hot_experts, replica_index, experts)
     codes = jnp.pad(codes.astype(bf16), ((0, quarter - here), (0, 0)))
-    gain_part = lax.dynamic_slice_in_dim(norm_gain, ep * block, block, 0)
-    router_part = lax.dynamic_slice_in_dim(router, ep * block, block, 0)
-    scaled = (hidden_part * gain_part[None, :]).astype(bf16)
-    square = jnp.sum(hidden_part * hidden_part, axis=1, keepdims=True)
-    logits = jnp.dot(scaled, router_part, preferred_element_type=f32)
-    wide = -(-(block + 2 + 3 * experts) // LANES) * LANES
-    extras = jnp.concatenate(
-        high_low(square)
-        + high_low(logits)
-        + [codes, jnp.zeros((quarter, wide - block - 2 - 3 * experts), bf16)],
-        axis=1,
-    )
-    paired = block % LANES == LANES // 2 == wide - block and n_ep // n_tp % 2 == 0
-    sent = jnp.concatenate([scaled, extras], axis=1)
+    count = n_y * n_ep
     if paired:
-        sent = jnp.where(ep % 2 == 0, sent, jnp.concatenate([extras, scaled], axis=1))
-    count = n_y * n_ep
+        sent = bundle(own, sum(others), gain_part, router_part, codes, count, wide)
+    else:
+        hidden_part = own + sum(others)
+        scaled = (hidden_part * gain_part).astype(bf16)
+        square = jnp.sum(hidden_part * hidden_part, axis=1, keepdims=True)
+        logits = jnp.dot(scaled, router_part.T, preferred_element_type=f32)
+        both = high_low(square) + high_low(logits)
+        sent = jnp.concatenate([scaled] + [b.astype(bf16) for b in both] + [codes], axis=1)
+        sent = jnp.pad(sent, ((0, 0), (0, wide - sent.shape[1])))
+        sent = jnp.broadcast_to(sent[None], (count, quarter, wide))
     mine = lax.all_to_all(
-        jnp.broadcast_to(sent[None], (count, quarter, wide)),
-        ("y", "ep"),
-        split_axis=0,
-        concat_axis=0,
-        tiled=True,
+        sent, ("y", "ep"), split_axis=0, concat_axis=0, tiled=True
     ).reshape(n_y, n_ep, quarter, wide)
     other = swap_cores(mine)
 
-    weights = (trainer_gate[0], trainer_up[0], trainer_down[0])
-    if paired and block % 16 == 0 and tokens <= 256:
-        keep, send = expert_block(mine, other, *weights, block, experts)
+    if paired:
+        keep, send = expert_block(mine, other, *weights[:2], fetch(weights[2])[0], block, experts)
     else:
         keep, send = expert_plain(ep, c, mine, other, *weights, block, experts)
 

time: 92.8 us -> 81 us (0.87)
  local copies, waits for them, and re-layouts: 15.5 us -> 3.28 us
  Pallas kernels: 5.93 us -> 10.1 us
  waiting for transfers between devices: 34.4 us -> 32.5 us
  matrix products: 1.87 us -> 0 us
    unnamed x31 -> x18, local copies, waits for them, and re-layouts: 12.9 us -> 1.38 us
    pallas_call x0 -> x3, Pallas kernels: none -> 2.67 us  [the longest x1 1.66 us: fetch(): pl.pallas_call(functools.partial(fetch_kernel, count), out_shape=tuple((j...]
    dot_general x3 -> x0, matrix products: 1.87 us -> none  [the longest x1 0.9 us: per_device(): logits = jnp.dot(scaled, router_part, preferred_element_type=f32)]
    pallas_call x1, Pallas kernels: 4.78 us -> 6.28 us  [attend(): pl.pallas_call(functools.partial(attend_kernel, steps, sub, block), grid=...]
    all_to_all x1, waiting for transfers between devices: 14.6 us -> 13.4 us  [per_device(): lax.all_to_all(parcel, 'ep', split_axis=0, concat_axis=0, tiled=True)]
    ppermute x2 -> x3, waiting for transfers between devices: 3.59 us -> 2.99 us  [swap_cores(): return lax.ppermute(block, 'c', [(0, 1), (1, 0)])]
    ppermute x2 -> x1, waiting for transfers between devices: 2.72 us -> 2.66 us  [exchange(): pieces.append(lax.ppermute(sent, axis, [(i, i ^ k) for i in range(size)]))]
  transfers between devices with their start and end apart: 6 -> 6, of which waited for: 6 -> 6; matrix products, arithmetic and copies ran while one was open for 3% -> 3% of each run, Pallas kernels for 0% -> 2%
where the time goes in v4:
time: 81 us; the launch traced here: 80.5 us
  waiting for transfers between devices  32.5 us (40%)
  blocking collectives  18.8 us (23%)
  starting transfers between devices  13.1 us (16%)
  Pallas kernels  10.1 us (12%)
  local copies, waits for them, and re-layouts  3.28 us (4%)
  other arithmetic  2.5 us (3%)
    all_to_all x1, blocking collectives, per_device(): lax.all_to_all(sent, ('y', 'ep'), split_axis=0, concat_axis=0, tiled=True)  18.8 us
    all_to_all x1, waiting for transfers between devices, per_device(): lax.all_to_all(outbound, ('y', 'ep'), split_axis=0, concat_axis=0, tiled=...  13.4 us
    all_to_all x1, waiting for transfers between devices, per_device(): lax.all_to_all(parcel, 'ep', split_axis=0, concat_axis=0, tiled=True)  13.4 us
    all_to_all x1, starting transfers between devices, per_device(): lax.all_to_all(parcel, 'ep', split_axis=0, concat_axis=0, tiled=True)  7.3 us
    pallas_call x1, Pallas kernels, attend(): pl.pallas_call(functools.partial(attend_kernel, steps, sub, block), grid=...  6.28 us
    all_to_all x1, starting transfers between devices, per_device(): lax.all_to_all(outbound, ('y', 'ep'), split_axis=0, concat_axis=0, tiled=...  3.59 us
    ppermute x3, waiting for transfers between devices, swap_cores(): return lax.ppermute(block, 'c', [(0, 1), (1, 0)])  2.99 us
    ppermute x1, waiting for transfers between devices, exchange(): pieces.append(lax.ppermute(sent, axis, [(i, i ^ k) for i in range(size)]))  2.66 us
  transfers between devices with their start and end apart: 6, of which 6 were waited for; matrix products, arithmetic and copies ran while one was open for 3% of the time, Pallas kernels for 2%

profile of v4, /device:TPU:0, one launch (start us, length us, event | category | flops | bytes accessed | tf_op | source)
XLA Modules:
  0.0 80.5 jit_solution(16148098238113636586)
XLA Ops:
  0.0 0.0 copy-start
  0.0 0.0 copy-start.4
  0.0 0.7 copy-done.4
  0.7 0.0 copy-start.5
  0.7 0.0 copy-start.7
  0.7 0.0 copy-start.8
  0.7 0.0 copy-start.6
  0.7 0.0 copy-start.1
  0.7 6.3 %attend.1 = bf16[8,16,2176]{2,1,0:T(8,128)(2,1)} custom-call(s32[16]{0:T(128)S(1)} %copy-done.4, bf16[16,16,512]{2,1,0:T(8,128)(2,1)} %ql.1, bf16[16,16,64]{2,1,0:T(8,128)(2,1)} %qr.1, bf16[16,256,512]{2,1,0:T(8,128)(2,1)} %cl.1, bf16[16,64,256]{2,1,0:T(8,128)(2,1)} %cr.1, bf16[16,3584]{1,0:T(8,128)(2,1)} %residual.1, bf16[16,512,128]{2,1,0:T(8,128)(2,1)} %vu_hbm.1), custom_call_target="tpu_custom_call" | custom-call | tf_op jit(solution)/shard_map/attend/pallas_call | solution.py:226
  7.0 7.3 %all-to-all-start = ((bf16[8,16,2176]{2,1,0:T(8,128)(2,1)}), bf16[8,16,2176]{2,1,0:T(8,128)(2,1)S(1)}, u32[]{:S(2)}, u32[]{:S(2)}) async-start(bf16[8,16,2176]{2,1,0:T(8,128)(2,1)} %attend.1), calls=%async_computation | async-start | bytes 1114112 | tf_op jit(solution)/shard_map/all_to_all | solution.py:415
  14.3 0.0 copy-done.5
  14.3 0.1 copy.21
  14.4 0.0 copy-done.7
  14.4 0.0 copy-done.8
  14.4 0.1 fusion.2
  14.5 0.1 convert_reduce_fusion.2
  14.6 0.0 copy-done.6
  14.6 0.2 fusion.1
  14.8 0.1 copy.20
  14.9 0.8 dynamic_slice.24
  15.6 0.4 convert_reduce_fusion.1
  16.1 13.4 %all-to-all-done = bf16[8,16,2176]{2,1,0:T(8,128)(2,1)S(1)} async-done(((bf16[8,16,2176]{2,1,0:T(8,128)(2,1)}), bf16[8,16,2176]{2,1,0:T(8,128)(2,1)S(1)}, u32[]{:S(2)}, u32[]{:S(2)}) %all-to-all-start) | async-done | bytes 557088 | tf_op jit(solution)/shard_map/all_to_all | solution.py:415
  29.5 0.0 copy-done.1
  29.5 0.7 project.1
  30.2 0.1 collective-permute-start
  30.3 1.3 %collective-permute-done = f32[2,32,448]{2,1,0:T(8,128)S(1)} collective-permute-done((f32[2,32,448]{2,1,0:T(8,128)S(1)}, f32[2,32,448]{2,1,0:T(8,128)S(1)}, u32[]{:S(2)}, u32[]{:S(2)}) %collective-permute-start) | collective-permute-done | bytes 114720 | tf_op jit(solution)/shard_map/ppermute | solution.py:375
  31.6 1.6 %collective-permute-start.1 = (f32[32,448]{1,0:T(8,128)S(1)}, f32[32,448]{1,0:T(8,128)S(1)}, u32[]{:S(2)}, u32[]{:S(2)}) collective-permute-start(f32[32,448]{1,0:T(8,128)S(1)} %get-tuple-element.13), channel_id=1, source_target_pairs={{0,2},{2,0},{1,3},{3,1},{4,6},{6,4},{5,7},{7,5},{8,10},{10,8},{9,1... | collective-permute-start | bytes 172040 | tf_op jit(solution)/shard_map/ppermute | solution.py:365
  33.2 0.0 copy-done
  33.2 0.1 dynamic-slice_bitcast_fusion.2.router_t
  33.3 2.7 %collective-permute-done.1.got = f32[32,448]{1,0:T(8,128)S(1)} collective-permute-done((f32[32,448]{1,0:T(8,128)S(1)}, f32[32,448]{1,0:T(8,128)S(1)}, u32[]{:S(2)}, u32[]{:S(2)}) %collective-permute-start.1) | collective-permute-done | bytes 57376 | tf_op jit(solution)/shard_map/ppermute | solution.py:365
  36.0 0.3 bundle.1
  36.3 18.8 %all_to_all.15 = bf16[16,32,512]{2,1,0:T(8,128)(2,1)S(1)} all-to-all(bf16[16,32,512]{2,1,0:T(8,128)(2,1)S(1)} %bundle.1), channel_id=1, replica_groups=mesh['ep'=8,'y'=2,'c'=2] {'y','ep'}, dimensions={0} | all-to-all | bytes 1048576 | tf_op jit(solution)/shard_map/all_to_all | solution.py:452
  55.1 0.0 collective-permute-start.2
  55.1 0.0 copy-start.2
  55.1 0.0 copy-start.3
  55.1 1.7 %fetch.1.down = bf16[256,3584]{1,0:T(8,128)(2,1)S(1)} custom-call(bf16[256,3584]{1,0:T(8,128)(2,1)} %bitcast.26), custom_call_target="tpu_custom_call" | custom-call | bytes 3670016 | tf_op jit(solution)/shard_map/fetch/pallas_call | solution.py:124
  56.8 0.2 collective-permute-done.2.other
  57.0 0.1 copy-done.2
  57.2 0.6 copy-done.3
  57.7 1.2 %experts.1 = (bf16[2,128,896]{2,1,0:T(8,128)(2,1)S(1)}, bf16[2,128,896]{2,1,0:T(8,128)(2,1)S(1)}) custom-call(bf16[2,8,32,512]{3,2,1,0:T(8,128)(2,1)S(1)} %bitcast.20, bf16[2,8,32,512]{3,2,1,0:T(8,128)(2,1)S(1)} %collective-permute-done.2.other, bf16[3584,256]{1,0:T(8,128)(2,1)S(1)} %bitcast.23, bf16[3584,256]{1,0:T(8,128)(2,1)S(1)} %bitcast.24, ...), custom_call_target="tpu_custom_call" | custom-call | tf_op jit(solution)/shard_map/experts/pallas_call | solution.py:327
  58.9 0.6 collective-permute-start.3
  59.5 1.4 %collective-permute-done.3 = bf16[2,128,896]{2,1,0:T(8,128)(2,1)S(1)} collective-permute-done((bf16[2,128,896]{2,1,0:T(8,128)(2,1)S(1)}, bf16[2,128,896]{2,1,0:T(8,128)(2,1)S(1)}, u32[]{:S(2)}, u32[]{:S(2)}) %collective-permute-start.3) | collective-permute-done | bytes 458784 | tf_op jit(solution)/shard_map/ppermute | solution.py:375
  60.9 0.9 %add_convert_fusion = bf16[2,128,896]{2,1,0:T(8,128)(2,1)} fusion(bf16[2,128,896]{2,1,0:T(8,128)(2,1)S(1)} %collective-permute-done.3, bf16[2,128,896]{2,1,0:T(8,128)(2,1)S(1)} %get-tuple-element.11), kind=kLoop, calls=%fused_computation.1 | loop fusion | flops 917504 | bytes 1376256 | tf_op jit(solution)/shard_map/convert_element_type | solution.py:463
  61.8 3.6 %all-to-all-start.2 = ((bf16[16,16,896]{2,1,0:T(8,128)(2,1)}), bf16[16,16,896]{2,1,0:T(8,128)(2,1)S(1)}, u32[]{:S(2)}, u32[]{:S(2)}) async-start(bf16[16,16,896]{2,1,0:T(8,128)(2,1)} %bitcast.12), calls=%async_computation.2 | async-start | bytes 917504 | tf_op jit(solution)/shard_map/all_to_all | solution.py:465
  65.5 0.8 dynamic_slice.28
  66.3 0.1 slice_bitcast_fusion.1
  66.3 13.4 %all-to-all-done.2 = bf16[16,16,896]{2,1,0:T(8,128)(2,1)S(1)} async-done(((bf16[16,16,896]{2,1,0:T(8,128)(2,1)}), bf16[16,16,896]{2,1,0:T(8,128)(2,1)S(1)}, u32[]{:S(2)}, u32[]{:S(2)}) %all-to-all-start.2) | async-done | bytes 458784 | tf_op jit(solution)/shard_map/all_to_all | solution.py:465
  79.8 0.1 convert_reduce_fusion
  79.8 0.7 add_convert_fusion.1
  (10 shorter events, 0.1 us)
Async XLA Ops:
  0.0 33.2 %copy-start = (bf16[3584,8]{0,1:T(8,128)(2,1)S(1)}, bf16[3584,8]{0,1:T(8,128)(2,1)}, u32[]{:S(2)}) copy-start(bf16[3584,8]{0,1:T(8,128)(2,1)} %param.26) | copy-start | bytes 172036
  0.0 0.7 copy-start.4
  0.7 13.6 %copy-start.5 = (s32[16,8]{0,1:T(8,128)S(1)}, s32[16,8]{0,1:T(8,128)}, u32[]{:S(2)}) copy-start(s32[16,8]{0,1:T(8,128)} %param.32) | copy-start | bytes 1540
  0.7 13.7 %copy-start.7 = (s32[2]{0:T(128)S(1)}, s32[2]{0:T(128)}, u32[]{:S(2)}) copy-start(s32[2]{0:T(128)} %param.30) | copy-start | bytes 28
  0.7 13.7 %copy-start.8 = (s32[8]{0:T(128)S(1)}, s32[8]{0:T(128)}, u32[]{:S(2)}) copy-start(s32[8]{0:T(128)} %param.31) | copy-start | bytes 100
  0.7 13.9 %copy-start.6 = (s32[16,8]{0,1:T(8,128)S(1)}, s32[16,8]{0,1:T(8,128)}, u32[]{:S(2)}) copy-start(s32[16,8]{0,1:T(8,128)} %param.33) | copy-start | bytes 1540
  0.7 28.8 %copy-start.1 = (bf16[448,2048]{1,0:T(8,128)(2,1)S(1)}, bf16[448,2048]{1,0:T(8,128)(2,1)}, u32[]{:S(2)}) copy-start(bf16[448,2048]{1,0:T(8,128)(2,1)} %out_proj.1) | copy-start | bytes 5505028
  7.0 22.5 %all-to-all-start = ((bf16[8,16,2176]{2,1,0:T(8,128)(2,1)}), bf16[8,16,2176]{2,1,0:T(8,128)(2,1)S(1)}, u32[]{:S(2)}, u32[]{:S(2)}) async-start(bf16[8,16,2176]{2,1,0:T(8,128)(2,1)} %attend.1), calls=%async_computation | async-start | bytes 1114112 | tf_op jit(solution)/shard_map/all_to_all | solution.py:415
  30.2 1.4 %collective-permute-start = (f32[2,32,448]{2,1,0:T(8,128)S(1)}, f32[2,32,448]{2,1,0:T(8,128)S(1)}, u32[]{:S(2)}, u32[]{:S(2)}) collective-permute-start(f32[2,32,448]{2,1,0:T(8,128)S(1)} %get-tuple-element.10), channel_id=1, source_target_pairs={{0,1},{1,0},{2,3},{3,2},{4,5},{5,4},{6,7},{7,6},{8,9},{9,8},{10,11... | collective-permute-start | bytes 344072 | tf_op jit(solution)/shard_map/ppermute | solution.py:375
  31.6 4.3 %collective-permute-start.1 = (f32[32,448]{1,0:T(8,128)S(1)}, f32[32,448]{1,0:T(8,128)S(1)}, u32[]{:S(2)}, u32[]{:S(2)}) collective-permute-start(f32[32,448]{1,0:T(8,128)S(1)} %get-tuple-element.13), channel_id=1, source_target_pairs={{0,2},{2,0},{1,3},{3,1},{4,6},{6,4},{5,7},{7,5},{8,10},{10,8},{9,1... | collective-permute-start | bytes 172040 | tf_op jit(solution)/shard_map/ppermute | solution.py:365
  55.1 1.9 %collective-permute-start.2 = (bf16[2,8,32,512]{3,2,1,0:T(8,128)(2,1)S(1)}, bf16[2,8,32,512]{3,2,1,0:T(8,128)(2,1)S(1)}, u32[]{:S(2)}, u32[]{:S(2)}) collective-permute-start(bf16[2,8,32,512]{3,2,1,0:T(8,128)(2,1)S(1)} %bitcast.19), channel_id=1, source_target_pairs={{0,1},{1,0},{2,3},{3,2},{4,5},{5,4},{6,7},{7,6},{8,9},{9,8},{10,11... | collective-permute-start | bytes 1572872 | tf_op jit(solution)/shard_map/ppermute | solution.py:375
  55.1 2.1 %copy-start.2 = (bf16[1,3584,256]{2,1,0:T(8,128)(2,1)S(1)}, bf16[1,3584,256]{2,1,0:T(8,128)(2,1)}, u32[]{:S(2)}) copy-start(bf16[1,3584,256]{2,1,0:T(8,128)(2,1)} %param.27) | copy-start | bytes 5505028
  55.1 2.6 %copy-start.3 = (bf16[1,3584,256]{2,1,0:T(8,128)(2,1)S(1)}, bf16[1,3584,256]{2,1,0:T(8,128)(2,1)}, u32[]{:S(2)}) copy-start(bf16[1,3584,256]{2,1,0:T(8,128)(2,1)} %param.28) | copy-start | bytes 5505028
  58.9 2.0 %collective-permute-start.3 = (bf16[2,128,896]{2,1,0:T(8,128)(2,1)S(1)}, bf16[2,128,896]{2,1,0:T(8,128)(2,1)S(1)}, u32[]{:S(2)}, u32[]{:S(2)}) collective-permute-start(bf16[2,128,896]{2,1,0:T(8,128)(2,1)S(1)} %get-tuple-element.12), channel_id=1, source_target_pairs={{0,1},{1,0},{2,3},{3,2},{4,5},{5,4},{6,7},{7,6},{8,9},{9,8},{10,11... | collective-permute-start | bytes 1376264 | tf_op jit(solution)/shard_map/ppermute | solution.py:375
  61.8 18.0 %all-to-all-start.2 = ((bf16[16,16,896]{2,1,0:T(8,128)(2,1)}), bf16[16,16,896]{2,1,0:T(8,128)(2,1)S(1)}, u32[]{:S(2)}, u32[]{:S(2)}) async-start(bf16[16,16,896]{2,1,0:T(8,128)(2,1)} %bitcast.12), calls=%async_computation.2 | async-start | bytes 917504 | tf_op jit(solution)/shard_map/all_to_all | solution.py:465
